TPU v7x, 256 devices: a whole 4x4x8 slice. The times are simulated.
256 devices in a mesh: table: 64 (over z, x, core), replica: 4 (over y).
Axes of the slice: x: 4, y: 4, z: 8, core: 2. Of those that a mesh axis runs over, the one named last changes fastest.
Arguments:
- emb_table: bfloat16 [65536, 128], P('table'), may hold values from -3 to 3
- cross_up: bfloat16 [256, 3456], replicated, may hold values from -0.375 to 0.375
- cross_down: bfloat16 [256, 3456], replicated, may hold values from -0.109375 to 0.109375
- cross_bias: float32 [3456], replicated, may hold values from -3 to 3
- out_weight: float32 [3456], replicated, may hold values from -0.109375 to 0.109375
- bottom_weight: float32 [13, 128], replicated, may hold values from -1.75 to 1.75
- bottom_bias: float32 [128], replicated, may hold values from -3 to 3
- dense_in: float32 [32768, 13], P(('table', 'replica')), may hold values from -6 to 6
- labels: int32 [32768], P(('table', 'replica')), may hold values from 0 to 1
- lookup_ids: int32 [32768, 26, 4], P(('table', 'replica')), may hold values from 0 to 6143
- bag_weight: float32 [32768, 26, 4], P(('table', 'replica')), may hold values from 0.25 to 1
- bag_length: int32 [32768, 26], P(('table', 'replica')), may hold values from 1 to 4
- want_blocks: int32 [64, 4, 64, 1], P('table', 'replica'), may hold values from 0 to 31
- hot_blocks: int32 [64, 2], P('table'), may hold values from 0 to 31
- hot_count: int32 [64], P('table'), may hold values from 1 to 2, as said below
Outputs:
- up_grad: float32 [256, 3456], P(('table', 'replica'))
- down_grad: float32 [256, 3456], P(('table', 'replica'))
- table_grad: float32 [65536, 128], P(('table', 'replica'))
Inputs may be any that keep to these rules, and one draw needn't show every extreme that they name: `hot_count`: each owner has 1 to 2 live hot slots, and some owner has 2.
All inputs are finite; a program needn't handle non-finite values.
Results may differ from a plain program's by a relative error of at most 0.0053.
Values may be sent and summed in bfloat16 or wider, within the bound.
No kernel may reach another device: no remote copies, remote signals or barrier semaphores. Data moves between devices by JAX's collectives and lax.ppermute only.
A program may use at most 64 MiB of HBM per device.

v0:
```python
import jax
import jax.numpy as jnp
from jax import lax
from jax.sharding import Mesh
from jax.sharding import PartitionSpec as P

EMB = 128
BLOCK = 32
TABLE = ("table_0", "table_1", "table_2")
TABLE_REPLICA = ("table_0", "table_1", "table_2", "replica")


def laid_out(blocks, dim):
    shape = list(blocks.shape[1:])
    shape[dim] *= blocks.shape[0]
    return jnp.moveaxis(blocks, 0, dim).reshape(shape)


def sent_to_all(x, axis):
    devices = lax.axis_size(axis)
    return lax.all_to_all(jnp.broadcast_to(x[None], (devices, *x.shape)), axis, 0, 0, tiled=True)


def gathered_copies(x, axis, dim):
    return laid_out(sent_to_all(x, axis), dim)


def split_up(x, dim, devices):
    shape = x.shape
    blocks = x.reshape(*shape[:dim], devices, shape[dim] // devices, *shape[dim + 1 :])
    return jnp.moveaxis(blocks, dim, 0)


def sent_and_summed(x, axis, dim):
    blocks = split_up(x, dim, lax.axis_size(axis))
    arrived = lax.all_to_all(blocks, axis, split_axis=0, concat_axis=0, tiled=True)
    return arrived.astype(jnp.float32).sum(axis=0)


def sent_and_summed_2(x, axis, dim):
    blocks = split_up(x, dim, lax.axis_size(axis))
    arrived = lax.all_to_all(blocks, axis, split_axis=0, concat_axis=0, tiled=True)
    return arrived.sum(axis=0)


def sum_in_two_steps(x, axes, dim):
    far, near = axes
    blocks = split_up(x, dim, lax.axis_size(far))
    nearer = sent_and_summed(blocks, near, dim + 1)
    arrived = lax.all_to_all(
        nearer.astype(jnp.bfloat16), far, split_axis=0, concat_axis=0, tiled=True
    )
    return arrived.astype(jnp.float32).sum(axis=0)


def sent_together(arrays, axis, dim, along):
    widths = [a.shape[along] for a in arrays]
    both = jnp.concatenate(arrays, axis=along)
    whole = sum_in_two_steps(both, axis, dim)
    return tuple(jnp.split(whole, [sum(widths[:k]) for k in range(1, len(widths))], axis=along))


def local_step(
    cached_rows,
    dense_dev,
    labels_dev,
    ids_dev,
    weight_dev,
    length_dev,
    cross_up,
    cross_down,
    cross_bias,
    out_weight,
    bottom_weight,
    bottom_bias,
):
    batch = ids_dev.shape[0]
    width = cached_rows.shape[1]
    gathered = cached_rows[ids_dev].astype(jnp.float32)
    slots = jnp.arange(ids_dev.shape[2], dtype=jnp.int32)
    bag_coef = jnp.where(
        slots[None, None, :] < length_dev[:, :, None], weight_dev, jnp.zeros((), jnp.float32)
    )
    pooled = jnp.sum(bag_coef[..., None] * gathered, axis=2)
    bottom = jax.nn.relu(
        jnp.dot(dense_dev, bottom_weight, precision=lax.Precision.HIGHEST) + bottom_bias
    )
    cross_base = jnp.concatenate([bottom, pooled.reshape(batch, -1)], 1).astype(jnp.bfloat16)
    low_rank = lax.dot_general(
        cross_base, cross_down, (((1,), (1,)), ((), ())), preferred_element_type=jnp.float32
    ).astype(jnp.bfloat16)
    cross_gate = jnp.dot(low_rank, cross_up, preferred_element_type=jnp.float32) + cross_bias
    base_wide = cross_base.astype(jnp.float32)
    crossed = base_wide * cross_gate + base_wide
    logits = jnp.dot(crossed, out_weight, precision=lax.Precision.HIGHEST)
    logit_grad = jax.nn.sigmoid(logits) - labels_dev.astype(jnp.float32)
    grad_crossed = logit_grad[:, None] * out_weight[None, :]
    g_cross = (grad_crossed * base_wide).astype(jnp.bfloat16)
    g_low = lax.dot_general(
        g_cross, cross_up, (((1,), (1,)), ((), ())), preferred_element_type=jnp.float32
    ).astype(jnp.bfloat16)
    up_part = lax.dot_general(
        low_rank, g_cross, (((0,), (0,)), ((), ())), preferred_element_type=jnp.float32
    )
    down_part = lax.dot_general(
        g_low, cross_base, (((0,), (0,)), ((), ())), preferred_element_type=jnp.float32
    )
    grad_base = grad_crossed * (cross_gate + 1.0) + jnp.dot(
        g_low, cross_down, preferred_element_type=jnp.float32
    )
    grad_pooled = grad_base[:, width:].reshape(batch, -1, width)
    contrib = bag_coef[..., None] * grad_pooled[:, :, None, :]
    cache_grad = (
        jnp.zeros(cached_rows.shape, jnp.float32)
        .at[ids_dev.reshape(-1)]
        .add(contrib.reshape(-1, width))
    )
    return (up_part, down_part, cache_grad)


def local(
    emb_table,
    cross_up,
    cross_down,
    cross_bias,
    out_weight,
    bottom_weight,
    bottom_bias,
    dense_in,
    labels,
    lookup_ids,
    bag_weight,
    bag_length,
    want_blocks,
    hot_blocks,
    hot_count,
):
    owners = lax.axis_size(TABLE)
    blocks = emb_table.reshape(-1, BLOCK, EMB)
    block_total = blocks.shape[0]
    wanted = want_blocks.reshape(owners, want_blocks.shape[3])
    asked_for = lax.all_to_all(wanted, TABLE, split_axis=0, concat_axis=0, tiled=True)
    served = blocks[asked_for]
    cold_rows = lax.all_to_all(served, TABLE, split_axis=0, concat_axis=0, tiled=True)
    slot_count = hot_blocks.shape[1]
    alive = jnp.arange(slot_count, dtype=jnp.int32) < hot_count[0]
    own_hot = jnp.where(alive[:, None, None], blocks[hot_blocks[0]], jnp.zeros((), jnp.bfloat16))
    replica_pos = lax.axis_index("replica")
    share_rows = BLOCK // lax.axis_size("replica")
    own_share = lax.dynamic_slice_in_dim(own_hot, replica_pos * share_rows, share_rows, 1)
    across = gathered_copies(own_share[:, None], TABLE, 1)
    hot_rows = gathered_copies(across, "replica", 2)
    cold_count = cold_rows.shape[0] * cold_rows.shape[1] * BLOCK
    cached_rows = jnp.concatenate([cold_rows.reshape(-1, EMB), hot_rows.reshape(-1, EMB)], 0)
    up_part, down_part, cache_grad = local_step(
        cached_rows,
        dense_in,
        labels,
        lookup_ids,
        bag_weight,
        bag_length,
        cross_up,
        cross_down,
        cross_bias,
        out_weight,
        bottom_weight,
        bottom_bias,
    )
    cold_grad = cache_grad[:cold_count].reshape(cold_rows.shape).astype(jnp.bfloat16)
    returned = lax.all_to_all(cold_grad, TABLE, split_axis=0, concat_axis=0, tiled=True)
    hot_grad = cache_grad[cold_count:].reshape(hot_rows.shape)
    by_rows = sent_and_summed(hot_grad.astype(jnp.bfloat16), "replica", 2)
    owned = sent_and_summed_2(by_rows, TABLE, 1)
    hot_sums = lax.dynamic_update_slice_in_dim(
        jnp.zeros(own_hot.shape, jnp.float32), owned[:, 0], replica_pos * share_rows, 1
    )
    block_ids = jnp.arange(block_total, dtype=jnp.int32)
    cold_pick = (asked_for.reshape(-1)[:, None] == block_ids[None, :]).astype(jnp.bfloat16)
    hot_pick = ((hot_blocks[0][:, None] == block_ids[None, :]) & alive[:, None]).astype(jnp.float32)
    block_grad = lax.dot_general(
        cold_pick,
        returned.reshape(cold_pick.shape[0], -1),
        (((0,), (0,)), ((), ())),
        preferred_element_type=jnp.float32,
    )
    block_grad = block_grad + lax.dot_general(
        hot_pick,
        hot_sums.reshape(slot_count, -1),
        (((0,), (0,)), ((), ())),
        precision=lax.Precision.HIGHEST,
    )
    table_grad = sent_and_summed_2(block_grad.reshape(-1, EMB), "replica", 0)
    up_grad, down_grad = sent_together(
        (up_part.astype(jnp.bfloat16), down_part.astype(jnp.bfloat16)),
        (("table_0", "table_1"), ("table_2", "replica")),
        0,
        1,
    )
    return (up_grad, down_grad, table_grad)


def solution(mesh):
    torus = Mesh(
        mesh.devices.reshape(8, 4, 2, mesh.shape["replica"]),
        ("table_0", "table_1", "table_2", "replica"),
    )
    in_specs = (
        P(TABLE, None),
        P(),
        P(),
        P(),
        P(),
        P(),
        P(),
        P(TABLE_REPLICA, None),
        P(TABLE_REPLICA),
        P(TABLE_REPLICA, None, None),
        P(TABLE_REPLICA, None, None),
        P(TABLE_REPLICA, None),
        P(TABLE, "replica", None, None),
        P(TABLE, None),
        P(TABLE),
    )
    out_specs = (P(TABLE_REPLICA, None), P(TABLE_REPLICA, None), P(TABLE_REPLICA, None))
    return jax.shard_map(local, mesh=torus, in_specs=in_specs, out_specs=out_specs, check_vma=False)
```

profile of v0, /device:TPU:32, one launch (start us, length us, event | category | flops | bytes accessed | tf_op | source)
XLA Modules:
  0.0 397.4 jit_solution(16118528666843343988)
XLA Ops:
  2.1 1.5 gather_fusion.1
  4.4 11.6 %all-to-all-start.2 = ((bf16[64,2,1,8,128]{4,3,1,2,0:T(8,128)(2,1)}), bf16[64,2,1,8,128]{4,3,1,2,0:T(8,128)(2,1)S(1)}, u32[]{:S(2)}, u32[]{:S(2)}) async-start(bf16[64,2,1,8,128]{4,3,1,2,0:T(8,128)(2,1)} %broadcast_in_dim.31), calls=%async_computation.2 | async-start | bytes 524288 | tf_op jit(solution)/shard_map/all_to_all | solution.py:21
  16.0 1.4 copy.75
  17.4 10.8 %all-to-all-done.2 = bf16[64,2,1,8,128]{4,3,1,2,0:T(8,128)(2,1)S(1)} async-done(((bf16[64,2,1,8,128]{4,3,1,2,0:T(8,128)(2,1)}), bf16[64,2,1,8,128]{4,3,1,2,0:T(8,128)(2,1)S(1)}, u32[]{:S(2)}, u32[]{:S(2)}) %all-to-all-start.2) | async-done | bytes 262176 | tf_op jit(solution)/shard_map/all_to_all | solution.py:21
  28.2 5.6 %all-to-all-start = ((s32[64,1,1]{2,1,0:T(1,128)}), s32[64,1,1]{2,1,0:T(1,128)S(1)}, u32[]{:S(2)}, u32[]{:S(2)}) async-start(s32[64,1,1]{2,1,0:T(1,128)} %copy.75), calls=%async_computation | async-start | bytes 65536 | tf_op jit(solution)/shard_map/all_to_all | solution.py:142
  33.9 3.7 copy.85
  37.6 2.2 reshape.146
  39.8 2.7 all-to-all-done
  43.6 4.6 %all-to-all-start.3 = ((bf16[4,2,64,8,128]{4,3,2,1,0:T(8,128)(2,1)}), bf16[4,2,64,8,128]{4,3,2,1,0:T(8,128)(2,1)S(1)}, u32[]{:S(2)}, u32[]{:S(2)}) async-start(bf16[4,2,64,8,128]{4,3,2,1,0:T(8,128)(2,1)} %broadcast_in_dim.33), calls=%async_computation.3 | async-start | bytes 2097152 | tf_op jit(solution)/shard_map/all_to_all | solution.py:21
  48.9 2.4 fusion.31
  51.3 1.4 gather_fusion
  52.7 10.6 %all-to-all-done.3 = bf16[4,2,64,8,128]{4,3,2,1,0:T(8,128)(2,1)S(1)} async-done(((bf16[4,2,64,8,128]{4,3,2,1,0:T(8,128)(2,1)}), bf16[4,2,64,8,128]{4,3,2,1,0:T(8,128)(2,1)S(1)}, u32[]{:S(2)}, u32[]{:S(2)}) %all-to-all-start.3) | async-done | bytes 1048608 | tf_op jit(solution)/shard_map/all_to_all | solution.py:21
  63.3 7.9 %all-to-all-start.1 = ((bf16[64,1,32,128]{3,2,1,0:T(8,128)(2,1)}), bf16[64,1,32,128]{3,2,1,0:T(8,128)(2,1)S(1)}, u32[]{:S(2)}, u32[]{:S(2)}) async-start(bf16[64,1,32,128]{3,2,1,0:T(8,128)(2,1)} %bitcast.2), calls=%async_computation.1 | async-start | bytes 1048576 | tf_op jit(solution)/shard_map/all_to_all | solution.py:144
  71.7 2.9 copy.74
  74.7 2.7 mul.62
  77.4 2.9 copy.78
  80.3 2.1 reshape.168
  82.4 1.1 copy.77
  83.5 4.4 %all-to-all-done.1 = bf16[64,1,32,128]{3,2,1,0:T(8,128)(2,1)S(1)} async-done(((bf16[64,1,32,128]{3,2,1,0:T(8,128)(2,1)}), bf16[64,1,32,128]{3,2,1,0:T(8,128)(2,1)S(1)}, u32[]{:S(2)}, u32[]{:S(2)}) %all-to-all-start.1) | async-done | bytes 524320 | tf_op jit(solution)/shard_map/all_to_all | solution.py:144
  88.7 1.5 pad_maximum_fusion
  90.2 47.1 %gather_fusion.2 = bf16[13312,128]{1,0:T(8,128)(2,1)} fusion(bf16[6144,128]{1,0:T(8,128)(2,1)S(1)} %pad_maximum_fusion, s32[13312]{0:T(1024)S(1)} %broadcast_clamp_fusion), kind=kCustom, calls=%fused_computation.2 | custom fusion | bytes 6868992 | tf_op jit(solution)/shard_map/gather | solution.py:79
  137.3 6.5 %fusion = bf16[128,26,128]{2,1,0:T(8,128)(2,1)S(1)} fusion(bf16[128,26,4,128]{3,2,1,0:T(4,128)(2,1)} %bitcast.71, f32[128,26,4]{2,1,0:T(8,128)} %copy.74), kind=kLoop, calls=%fused_computation.5 | loop fusion | flops 4685824 | bytes 4313088 | tf_op jit(solution)/shard_map/reduce_sum | solution.py:84
  145.4 2.2 convolution_convert_fusion.3
  148.3 1.6 fusion.14
  150.8 1.3 copy-done.3
  152.5 1.5 slice_add_fusion
  154.0 1.8 copy.87
  155.8 2.2 copy.88
  158.0 5.7 %mul.66 = f32[128,26,4,128]{3,2,1,0:T(4,128)} broadcast(f32[128,26,128]{2,1,0:T(8,128)} %copy.88), dimensions={0,1,3} | broadcast | bytes 8519680 | tf_op jit(solution)/shard_map/mul | solution.py:112
  163.8 80.3 %scatter_custom_fusion = f32[6144,128]{1,0:T(8,128)} fusion(s32[13312]{0:T(1024)} %bitcast.86, f32[13312,128]{1,0:T(8,128)} %bitcast.69, f32[13312]{0:T(1024)S(1)} %copy-done.5, f32[]{:T(128)} %constant.8.clone.1), kind=kCustom, calls=%fused_computation.6 | custom fusion | flops 3407872 | bytes 10015232 | tf_op jit(solution)/shard_map/scatter-add | solution.py:116
  244.1 2.0 convert.14
  246.2 1.2 copy.90
  247.4 4.2 %all-to-all-start.7 = ((bf16[4,2,64,8,128]{4,3,2,1,0:T(8,128)(2,1)}), bf16[4,2,64,8,128]{4,3,2,1,0:T(8,128)(2,1)}, u32[]{:S(2)}, u32[]{:S(2)}) async-start(bf16[4,2,64,8,128]{4,3,2,1,0:T(8,128)(2,1)} %copy.90), calls=%async_computation.7 | async-start | bytes 2097152 | tf_op jit(solution)/shard_map/all_to_all | solution.py:36
  252.5 15.2 %all-to-all-done.7 = bf16[4,2,64,8,128]{4,3,2,1,0:T(8,128)(2,1)} async-done(((bf16[4,2,64,8,128]{4,3,2,1,0:T(8,128)(2,1)}), bf16[4,2,64,8,128]{4,3,2,1,0:T(8,128)(2,1)}, u32[]{:S(2)}, u32[]{:S(2)}) %all-to-all-start.7) | async-done | bytes 1048608 | tf_op jit(solution)/shard_map/all_to_all | solution.py:36
  267.7 6.0 %all-to-all-start.6 = ((bf16[64,1,32,128]{3,2,1,0:T(8,128)(2,1)}), bf16[64,1,32,128]{3,2,1,0:T(8,128)(2,1)S(1)}, u32[]{:S(2)}, u32[]{:S(2)}) async-start(bf16[64,1,32,128]{3,2,1,0:T(8,128)(2,1)} %bitcast.79), calls=%async_computation.6 | async-start | bytes 1048576 | tf_op jit(solution)/shard_map/all_to_all | solution.py:170
  274.4 1.4 convert_reduce_fusion
  276.7 13.7 %all-to-all-done.6 = bf16[64,1,32,128]{3,2,1,0:T(8,128)(2,1)S(1)} async-done(((bf16[64,1,32,128]{3,2,1,0:T(8,128)(2,1)}), bf16[64,1,32,128]{3,2,1,0:T(8,128)(2,1)S(1)}, u32[]{:S(2)}, u32[]{:S(2)}) %all-to-all-start.6) | async-done | bytes 524320 | tf_op jit(solution)/shard_map/all_to_all | solution.py:170
  290.4 6.9 %all-to-all-start.8 = ((f32[64,2,1,8,128]{4,3,1,2,0:T(8,128)}), f32[64,2,1,8,128]{4,3,1,2,0:T(8,128)}, u32[]{:S(2)}, u32[]{:S(2)}) async-start(f32[64,2,1,8,128]{4,3,1,2,0:T(8,128)} %copy.91), calls=%async_computation.8 | async-start | bytes 1048576 | tf_op jit(solution)/shard_map/all_to_all | solution.py:42
  298.2 2.3 copy.105
  300.5 13.3 %all-to-all-done.8 = f32[64,2,1,8,128]{4,3,1,2,0:T(8,128)} async-done(((f32[64,2,1,8,128]{4,3,1,2,0:T(8,128)}), f32[64,2,1,8,128]{4,3,1,2,0:T(8,128)}, u32[]{:S(2)}, u32[]{:S(2)}) %all-to-all-start.8) | async-done | bytes 524320 | tf_op jit(solution)/shard_map/all_to_all | solution.py:42
  313.9 4.6 %all-to-all-start.4 = ((bf16[8,32,1,6912]{3,1,2,0:T(8,128)(2,1)}), bf16[8,32,1,6912]{3,1,2,0:T(8,128)(2,1)}, u32[]{:S(2)}, u32[]{:S(2)}) async-start(bf16[8,32,1,6912]{3,1,2,0:T(8,128)(2,1)} %bitcast.70), calls=%async_computation.4 | async-start | bytes 7077888 | tf_op jit(solution)/shard_map/all_to_all | solution.py:36
  318.9 1.1 reduce_sum.67
  321.4 39.1 %all-to-all-done.4 = bf16[8,32,1,6912]{3,1,2,0:T(8,128)(2,1)} async-done(((bf16[8,32,1,6912]{3,1,2,0:T(8,128)(2,1)}), bf16[8,32,1,6912]{3,1,2,0:T(8,128)(2,1)}, u32[]{:S(2)}, u32[]{:S(2)}) %all-to-all-start.4) | async-done | bytes 3538976 | tf_op jit(solution)/shard_map/all_to_all | solution.py:36
  360.5 3.5 all-to-all-start.9
  364.0 2.6 reduce_sum.62
  368.8 5.2 %all-to-all-done.9 = f32[4,256,128]{2,1,0:T(8,128)S(1)} async-done(((f32[4,256,128]{2,1,0:T(8,128)}), f32[4,256,128]{2,1,0:T(8,128)S(1)}, u32[]{:S(2)}, u32[]{:S(2)}) %all-to-all-start.9) | async-done | bytes 524320 | tf_op jit(solution)/shard_map/all_to_all | solution.py:42
  374.1 6.3 %all-to-all-start.5 = ((bf16[32,2,3456]{2,1,0:T(2,128)(2,1)}), bf16[32,2,3456]{2,1,0:T(2,128)(2,1)S(1)}, u32[]{:S(2)}, u32[]{:S(2)}) async-start(bf16[32,2,3456]{2,1,0:T(2,128)(2,1)} %reshape.191), calls=%async_computation.5 | async-start | bytes 884736 | tf_op jit(solution)/shard_map/all_to_all | solution.py:50
  381.1 14.5 %all-to-all-done.5 = bf16[32,2,3456]{2,1,0:T(2,128)(2,1)S(1)} async-done(((bf16[32,2,3456]{2,1,0:T(2,128)(2,1)}), bf16[32,2,3456]{2,1,0:T(2,128)(2,1)S(1)}, u32[]{:S(2)}, u32[]{:S(2)}) %all-to-all-start.5) | async-done | bytes 442400 | tf_op jit(solution)/shard_map/all_to_all | solution.py:50
  (72 shorter events, 18.1 us)
Async XLA Ops:
  0.6 147.0 %copy-start = (bf16[256,3456]{1,0:T(8,128)(2,1)S(1)}, bf16[256,3456]{1,0:T(8,128)(2,1)}, u32[]{:S(2)}) copy-start(bf16[256,3456]{1,0:T(8,128)(2,1)} %param.16) | copy-start | bytes 5308420
  4.4 23.8 %all-to-all-start.2 = ((bf16[64,2,1,8,128]{4,3,1,2,0:T(8,128)(2,1)}), bf16[64,2,1,8,128]{4,3,1,2,0:T(8,128)(2,1)S(1)}, u32[]{:S(2)}, u32[]{:S(2)}) async-start(bf16[64,2,1,8,128]{4,3,1,2,0:T(8,128)(2,1)} %broadcast_in_dim.31), calls=%async_computation.2 | async-start | bytes 524288 | tf_op jit(solution)/shard_map/all_to_all | solution.py:21
  28.2 14.2 %all-to-all-start = ((s32[64,1,1]{2,1,0:T(1,128)}), s32[64,1,1]{2,1,0:T(1,128)S(1)}, u32[]{:S(2)}, u32[]{:S(2)}) async-start(s32[64,1,1]{2,1,0:T(1,128)} %copy.75), calls=%async_computation | async-start | bytes 65536 | tf_op jit(solution)/shard_map/all_to_all | solution.py:142
  39.8 9.1 %copy-start.7 = (f32[3456]{0:T(1024)S(1)}, f32[3456]{0:T(1024)}, u32[]{:S(2)}) copy-start(f32[3456]{0:T(1024)} %param.19) | copy-start | bytes 41476
  39.8 11.5 %copy-start.4 = (bf16[1024,128]{1,0:T(8,128)(2,1)S(1)}, bf16[1024,128]{1,0:T(8,128)(2,1)}, u32[]{:S(2)}) copy-start(bf16[1024,128]{1,0:T(8,128)(2,1)} %param.15) | copy-start | bytes 786436
  43.6 27.7 %copy-start.13 = (f32[128,13]{0,1:T(8,128)S(1)}, f32[128,13]{0,1:T(8,128)}, u32[]{:S(2)}) copy-start(f32[128,13]{0,1:T(8,128)} %param.22) | copy-start | bytes 19972
  43.6 27.7 %copy-start.14 = (f32[13,128]{1,0:T(8,128)S(1)}, f32[13,128]{1,0:T(8,128)}, u32[]{:S(2)}) copy-start(f32[13,128]{1,0:T(8,128)} %param.20) | copy-start | bytes 19972
  43.6 27.7 %copy-start.15 = (f32[128]{0:T(128)S(1)}, f32[128]{0:T(128)}, u32[]{:S(2)}) copy-start(f32[128]{0:T(128)} %param.21) | copy-start | bytes 1540
  43.6 28.1 %copy-start.8 = (f32[128,26,4]{0,2,1:T(4,128)S(1)}, f32[128,26,4]{0,2,1:T(4,128)}, u32[]{:S(2)}) copy-start(f32[128,26,4]{0,2,1:T(4,128)} %param.25) | copy-start | bytes 159748
  43.6 28.1 %copy-start.10 = (s32[128,26]{0,1:T(8,128)S(1)}, s32[128,26]{0,1:T(8,128)}, u32[]{:S(2)}) copy-start(s32[128,26]{0,1:T(8,128)} %param.26) | copy-start | bytes 39940
  43.6 19.7 %all-to-all-start.3 = ((bf16[4,2,64,8,128]{4,3,2,1,0:T(8,128)(2,1)}), bf16[4,2,64,8,128]{4,3,2,1,0:T(8,128)(2,1)S(1)}, u32[]{:S(2)}, u32[]{:S(2)}) async-start(bf16[4,2,64,8,128]{4,3,2,1,0:T(8,128)(2,1)} %broadcast_in_dim.33), calls=%async_computation.3 | async-start | bytes 2097152 | tf_op jit(solution)/shard_map/all_to_all | solution.py:21
  63.3 24.6 %all-to-all-start.1 = ((bf16[64,1,32,128]{3,2,1,0:T(8,128)(2,1)}), bf16[64,1,32,128]{3,2,1,0:T(8,128)(2,1)S(1)}, u32[]{:S(2)}, u32[]{:S(2)}) async-start(bf16[64,1,32,128]{3,2,1,0:T(8,128)(2,1)} %bitcast.2), calls=%async_computation.1 | async-start | bytes 1048576 | tf_op jit(solution)/shard_map/all_to_all | solution.py:144
  71.7 5.6 %copy-start.6 = (s32[128,26,4]{0,2,1:T(4,128)S(1)}, s32[128,26,4]{0,2,1:T(4,128)}, u32[]{:S(2)}) copy-start(s32[128,26,4]{0,2,1:T(4,128)} %param.24) | copy-start | bytes 159748
  87.9 0.8 copy-start.2
  145.4 2.2 copy-start.9
  147.6 0.7 copy-start.12
  150.6 1.5 copy-start.3
  158.0 5.7 %copy-start.5 = (f32[13312]{0:T(1024)S(1)}, f32[13312]{0:T(1024)}, u32[]{:S(2)}) copy-start(f32[13312]{0:T(1024)} %mul.62) | copy-start | bytes 159748
  247.4 20.3 %all-to-all-start.7 = ((bf16[4,2,64,8,128]{4,3,2,1,0:T(8,128)(2,1)}), bf16[4,2,64,8,128]{4,3,2,1,0:T(8,128)(2,1)}, u32[]{:S(2)}, u32[]{:S(2)}) async-start(bf16[4,2,64,8,128]{4,3,2,1,0:T(8,128)(2,1)} %copy.90), calls=%async_computation.7 | async-start | bytes 2097152 | tf_op jit(solution)/shard_map/all_to_all | solution.py:36
  267.7 22.7 %all-to-all-start.6 = ((bf16[64,1,32,128]{3,2,1,0:T(8,128)(2,1)}), bf16[64,1,32,128]{3,2,1,0:T(8,128)(2,1)S(1)}, u32[]{:S(2)}, u32[]{:S(2)}) async-start(bf16[64,1,32,128]{3,2,1,0:T(8,128)(2,1)} %bitcast.79), calls=%async_computation.6 | async-start | bytes 1048576 | tf_op jit(solution)/shard_map/all_to_all | solution.py:170
  290.4 23.5 %all-to-all-start.8 = ((f32[64,2,1,8,128]{4,3,1,2,0:T(8,128)}), f32[64,2,1,8,128]{4,3,1,2,0:T(8,128)}, u32[]{:S(2)}, u32[]{:S(2)}) async-start(f32[64,2,1,8,128]{4,3,1,2,0:T(8,128)} %copy.91), calls=%async_computation.8 | async-start | bytes 1048576 | tf_op jit(solution)/shard_map/all_to_all | solution.py:42
  313.9 6.1 %copy-start.11 = (s32[1,2]{1,0:T(1,128)S(1)}, s32[1,2]{1,0:T(1,128)}, u32[]{:S(2)}) copy-start(s32[1,2]{1,0:T(1,128)} %param.28) | copy-start | bytes 28
  313.9 46.6 %all-to-all-start.4 = ((bf16[8,32,1,6912]{3,1,2,0:T(8,128)(2,1)}), bf16[8,32,1,6912]{3,1,2,0:T(8,128)(2,1)}, u32[]{:S(2)}, u32[]{:S(2)}) async-start(bf16[8,32,1,6912]{3,1,2,0:T(8,128)(2,1)} %bitcast.70), calls=%async_computation.4 | async-start | bytes 7077888 | tf_op jit(solution)/shard_map/all_to_all | solution.py:36
  360.5 13.6 %all-to-all-start.9 = ((f32[4,256,128]{2,1,0:T(8,128)}), f32[4,256,128]{2,1,0:T(8,128)S(1)}, u32[]{:S(2)}, u32[]{:S(2)}) async-start(f32[4,256,128]{2,1,0:T(8,128)} %reshape_reshape.11), calls=%async_computation.9 | async-start | bytes 1048576 | tf_op jit(solution)/shard_map/all_to_all | solution.py:42
  368.0 29.5 %copy-start.1 = (bf16[256,3456]{1,0:T(8,128)(2,1)S(1)}, bf16[256,3456]{1,0:T(8,128)(2,1)}, u32[]{:S(2)}) copy-start(bf16[256,3456]{1,0:T(8,128)(2,1)} %param.16) | copy-start | bytes 5308420
  374.1 21.5 %all-to-all-start.5 = ((bf16[32,2,3456]{2,1,0:T(2,128)(2,1)}), bf16[32,2,3456]{2,1,0:T(2,128)(2,1)S(1)}, u32[]{:S(2)}, u32[]{:S(2)}) async-start(bf16[32,2,3456]{2,1,0:T(2,128)(2,1)} %reshape.191), calls=%async_computation.5 | async-start | bytes 884736 | tf_op jit(solution)/shard_map/all_to_all | solution.py:50
where the time goes:
time: 399 us; the launch traced here: 397 us
  waiting for transfers between devices  130 us (33%)
  other arithmetic  104 us (26%)
  local copies, waits for them, and re-layouts  93.2 us (23%)
  starting transfers between devices  61.3 us (15%)
  matrix products  7.86 us (2%)
    scatter-add x1, other arithmetic, local_step(): cache_grad = jnp.zeros(cached_rows.shape, jnp.float32).at[ids_dev.reshape...  80.3 us
    all_to_all x2, waiting for transfers between devices, sent_and_summed(): lax.all_to_all(blocks, axis, split_axis=0, concat_axis=0, tiled=True)  54.3 us
    gather x1, local copies, waits for them, and re-layouts, local_step(): gathered = cached_rows[ids_dev].astype(jnp.float32)  47.1 us
    all_to_all x2, waiting for transfers between devices, sent_to_all(): lax.all_to_all(jnp.broadcast_to(x[None], (devices, *x.shape)), axis, 0, 0...  21.4 us
    all_to_all x2, waiting for transfers between devices, sent_and_summed_2(): lax.all_to_all(blocks, axis, split_axis=0, concat_axis=0, tiled=True)  18.6 us
    all_to_all x2, starting transfers between devices, sent_to_all(): lax.all_to_all(jnp.broadcast_to(x[None], (devices, *x.shape)), axis, 0, 0...  16.2 us
    all_to_all x1, waiting for transfers between devices, sum_in_two_steps(): lax.all_to_all(nearer.astype(jnp.bfloat16), far, split_axis=0, concat_axi...  14.5 us
    all_to_all x1, waiting for transfers between devices, local(): lax.all_to_all(cold_grad, TABLE, split_axis=0, concat_axis=0, tiled=True)  13.7 us
  transfers between devices with their start and end apart: 10, of which 10 were waited for; matrix products, arithmetic and copies ran while one was open for 10% of the time, Pallas kernels for 0%

commit v1 on v0

v1 whole, which is shorter than its diff:
```python
import functools

import jax
import jax.numpy as jnp
from jax import lax
from jax.experimental import pallas as pl
from jax.experimental.pallas import tpu as pltpu
from jax.sharding import Mesh
from jax.sharding import PartitionSpec as P

EMB = 128
BLOCK = 32
TABLE = ("table_0", "table_1", "table_2")
TABLE_REPLICA = ("table_0", "table_1", "table_2", "replica")
BF = jnp.bfloat16
F32 = jnp.float32


def build_kernel(first, tile, slots_ref, iota_ref, out_ref):
    base = (first + pl.program_id(0) * tile).astype(F32)
    feats, _, batch = slots_ref.shape
    rows = iota_ref[...]

    def one(f, carry):
        packed = slots_ref[f]
        rel = jnp.clip(packed[:4] - base, -1.0, float(tile)).astype(BF)
        coef = packed[4:].astype(BF)
        acc = jnp.zeros((tile, batch), BF)
        for s in range(4):
            hit = rows == jnp.broadcast_to(rel[s : s + 1], (tile, batch))
            acc = jnp.where(hit, jnp.broadcast_to(coef[s : s + 1], (tile, batch)), acc)
        out_ref[:, pl.ds(pl.multiple_of(f * batch, batch), batch)] = acc
        return carry

    lax.fori_loop(0, feats, one, 0)


def build_selection(slots, first, count):
    tile = 256
    feats, _, batch = slots.shape
    bags = feats * batch
    iota = lax.broadcasted_iota(jnp.int32, (tile, batch), 0).astype(BF)
    return pl.pallas_call(
        functools.partial(build_kernel, first, tile),
        grid=(count // tile,),
        in_specs=[
            pl.BlockSpec((feats, 8, batch), lambda i: (0, 0, 0)),
            pl.BlockSpec((tile, batch), lambda i: (0, 0)),
        ],
        out_specs=pl.BlockSpec((tile, bags), lambda i: (i, 0)),
        out_shape=jax.ShapeDtypeStruct((count, bags), BF),
        cost_estimate=pl.CostEstimate(
            flops=count * bags * 8, bytes_accessed=count * bags * 2, transcendentals=0
        ),
        name="build_selection",
    )(slots, iota)


def gather_kernel(rows_ref, sel_ref, out_ref):
    part = lax.dot_general(
        rows_ref[...], sel_ref[...], (((0,), (0,)), ((), ())), preferred_element_type=F32
    )

    @pl.when(pl.program_id(0) == 0)
    def _():
        out_ref[...] = part

    @pl.when(pl.program_id(0) > 0)
    def _():
        out_ref[...] += part


def gather_pooled(rows, sel):
    tile = 512
    count, bags = sel.shape
    return pl.pallas_call(
        gather_kernel,
        grid=(count // tile,),
        in_specs=[
            pl.BlockSpec((tile, EMB), lambda i: (i, 0)),
            pl.BlockSpec((tile, bags), lambda i: (i, 0)),
        ],
        out_specs=pl.BlockSpec((EMB, bags), lambda i: (0, 0)),
        out_shape=jax.ShapeDtypeStruct((EMB, bags), F32),
        cost_estimate=pl.CostEstimate(
            flops=2 * count * bags * EMB, bytes_accessed=count * bags * 2, transcendentals=0
        ),
        name="gather_pooled",
    )(rows, sel)


def cross_kernel(
    rows_ref,
    sel_ref,
    hot_ref,
    scale_ref,
    scale_t_ref,
    bottom_ref,
    labels_ref,
    up_ref,
    down_ref,
    bias_ref,
    ow_ref,
    lines_ref,
    gpool_ref,
    acc,
    base_ref,
):
    step = pl.program_id(0)
    part = lax.dot_general(
        rows_ref[...], sel_ref[...], (((0,), (0,)), ((), ())), preferred_element_type=F32
    )

    @pl.when(step == 0)
    def _():
        acc[...] = hot_ref[...] + part

    @pl.when(step > 0)
    def _():
        acc[...] += part

    @pl.when(step == pl.num_programs(0) - 1)
    def _():
        batch = bottom_ref.shape[0]
        width = up_ref.shape[1]
        feats = width // EMB - 1
        base_ref[:, :EMB] = bottom_ref[...].astype(BF)
        for f in range(feats):
            block = acc[:, f * batch : (f + 1) * batch]
            base_ref[:, (f + 1) * EMB : (f + 2) * EMB] = (block * scale_ref[f : f + 1, :]).T.astype(BF)
        base = base_ref[...]
        nt = (((1,), (1,)), ((), ()))
        tn = (((0,), (0,)), ((), ()))
        low = lax.dot_general(base, down_ref[...], nt, preferred_element_type=F32).astype(BF)
        wide = base.astype(F32)
        ow = ow_ref[...]
        gate = jnp.dot(low, up_ref[...], preferred_element_type=F32) + bias_ref[...]
        crossed = wide * gate + wide
        logits = jnp.sum(crossed * ow, axis=1, keepdims=True)
        lg = jax.nn.sigmoid(logits) - labels_ref[...].astype(F32)
        grad_crossed = lg * ow
        g_cross = (grad_crossed * wide).astype(BF)
        g_low = lax.dot_general(g_cross, up_ref[...], nt, preferred_element_type=F32).astype(BF)
        up_part = lax.dot_general(low, g_cross, tn, preferred_element_type=F32)
        down_part = lax.dot_general(g_low, base, tn, preferred_element_type=F32)
        rank, per = up_part.shape[0], feats + 1
        lines = lines_ref.shape[0] // rank
        for c in range(per):
            lines_ref[pl.ds(c, rank, stride=lines), :] = up_part[:, c * EMB : (c + 1) * EMB]
            lines_ref[pl.ds(per + c, rank, stride=lines), :] = down_part[
                :, c * EMB : (c + 1) * EMB
            ]
        for c in range(2 * per, lines):
            lines_ref[pl.ds(c, rank, stride=lines), :] = jnp.zeros((rank, EMB), F32)
        grad_base = grad_crossed * (gate + 1.0) + jnp.dot(
            g_low, down_ref[...], preferred_element_type=F32
        )
        for f in range(feats):
            block = grad_base[:, (f + 1) * EMB : (f + 2) * EMB] * scale_t_ref[:, f : f + 1]
            gpool_ref[f * batch : (f + 1) * batch, :] = block.astype(BF)


def cross_layer(rows, sel, pooled_hot, scale, bottom, labels, up, down, bias, ow):
    tile = 512
    count, bags = sel.shape
    rank, width = up.shape
    batch = bottom.shape[0]
    lines = rank * pl.cdiv(2 * width // EMB, 8) * 8
    whole = lambda *shape: pl.BlockSpec(shape, lambda i: (0,) * len(shape))
    return pl.pallas_call(
        cross_kernel,
        grid=(count // tile,),
        in_specs=[
            pl.BlockSpec((tile, EMB), lambda i: (i, 0)),
            pl.BlockSpec((tile, bags), lambda i: (i, 0)),
            whole(EMB, bags),
            whole(*scale.shape),
            whole(batch, scale.shape[0]),
            whole(batch, EMB),
            whole(batch, 1),
            whole(rank, width),
            whole(rank, width),
            whole(1, width),
            whole(1, width),
        ],
        out_specs=[whole(lines, EMB), whole(bags, EMB)],
        out_shape=[
            jax.ShapeDtypeStruct((lines, EMB), F32),
            jax.ShapeDtypeStruct((bags, EMB), BF),
        ],
        scratch_shapes=[
            pltpu.VMEM((EMB, bags), F32),
            pltpu.VMEM((batch, width), BF),
        ],
        cost_estimate=pl.CostEstimate(
            flops=2 * count * bags * EMB + 12 * batch * rank * width,
            bytes_accessed=count * bags * 2 + 8 * rank * width,
            transcendentals=batch,
        ),
        name="cross_layer",
    )(rows, sel, pooled_hot, scale, scale.T, bottom, labels, up, down, bias, ow)


def scatter_kernel(sel_ref, grad_ref, out_ref):
    out_ref[...] = jnp.dot(
        sel_ref[...], grad_ref[...], preferred_element_type=F32
    ).astype(out_ref.dtype)


def scatter_rows(sel, grad, dtype):
    tile = 512
    count, bags = sel.shape
    return pl.pallas_call(
        scatter_kernel,
        grid=(count // tile,),
        in_specs=[
            pl.BlockSpec((tile, bags), lambda i: (i, 0)),
            pl.BlockSpec((bags, EMB), lambda i: (0, 0)),
        ],
        out_specs=pl.BlockSpec((tile, EMB), lambda i: (i, 0)),
        out_shape=jax.ShapeDtypeStruct((count, EMB), dtype),
        cost_estimate=pl.CostEstimate(
            flops=2 * count * bags * EMB, bytes_accessed=count * bags * 2, transcendentals=0
        ),
        name="scatter_rows",
    )(sel, grad)


def hot_kernel(count_ref, picks_ref, block_ref, out_ref):
    live = pl.program_id(0) < count_ref[0]
    rows = block_ref[...]
    out_ref[...] = jnp.where(live, rows, jnp.zeros_like(rows))


def own_hot_rows(emb_table, picks, count):
    slots = picks.shape[0]
    return pl.pallas_call(
        hot_kernel,
        grid_spec=pltpu.PrefetchScalarGridSpec(
            num_scalar_prefetch=2,
            grid=(slots,),
            in_specs=[pl.BlockSpec((BLOCK, EMB), lambda s, count, picks: (picks[s], 0))],
            out_specs=pl.BlockSpec((BLOCK, EMB), lambda s, count, picks: (s, 0)),
        ),
        out_shape=jax.ShapeDtypeStruct((slots * BLOCK, EMB), BF),
        name="own_hot_rows",
    )(count, picks, emb_table)


def serve_kernel(picks_ref, table_ref, out_ref):
    for i in range(out_ref.shape[0]):
        start = pl.multiple_of(picks_ref[i] * BLOCK, BLOCK)
        out_ref[i] = table_ref[pl.ds(start, BLOCK), :]


def served_blocks(emb_table, picks):
    owners = picks.shape[0]
    return pl.pallas_call(
        serve_kernel,
        in_specs=[
            pl.BlockSpec(memory_space=pltpu.SMEM),
            pl.BlockSpec(memory_space=pltpu.VMEM),
        ],
        out_shape=jax.ShapeDtypeStruct((owners, BLOCK, EMB), BF),
        name="served_blocks",
    )(picks, emb_table)


def collect_kernel(picks_ref, hot_picks_ref, count_ref, back_ref, hot_ref, out_ref, acc):
    acc[...] = jnp.zeros_like(acc)
    for i in range(back_ref.shape[0]):
        start = pl.multiple_of(picks_ref[i] * BLOCK, BLOCK)
        acc[pl.ds(start, BLOCK), :] += back_ref[i].astype(F32)
    for s in range(hot_picks_ref.shape[0]):
        start = pl.multiple_of(hot_picks_ref[s] * BLOCK, BLOCK)
        hot = hot_ref[s * BLOCK : (s + 1) * BLOCK, :]
        acc[pl.ds(start, BLOCK), :] += jnp.where(s < count_ref[0], hot, jnp.zeros_like(hot))
    out_ref[...] = acc[...].astype(out_ref.dtype)


def collected(rows, picks, hot_picks, count, back, hot):
    smem = pl.BlockSpec(memory_space=pltpu.SMEM)
    vmem = pl.BlockSpec(memory_space=pltpu.VMEM)
    return pl.pallas_call(
        collect_kernel,
        in_specs=[smem, smem, smem, vmem, vmem],
        out_shape=jax.ShapeDtypeStruct((rows, EMB), BF),
        scratch_shapes=[pltpu.VMEM((rows, EMB), F32)],
        name="collected",
    )(picks, hot_picks, count, back, hot)


def slots_kernel(cold, hot_slots, tries, ids_ref, weight_ref, length_ref, slots_ref, scale_ref):
    bag = ids_ref.shape[0]
    length = length_ref[...]
    row_bits = BLOCK.bit_length() - 1
    cold_bits = cold.bit_length() - 1
    ids, coef = [], []
    for s in range(bag):
        i = ids_ref[s]
        h = i - cold
        slot, rest = h >> cold_bits, h & (cold - 1)
        moved = cold + ((rest >> row_bits) * hot_slots + slot) * BLOCK + (rest & (BLOCK - 1))
        ids.append(jnp.where(i < cold, i, moved))
        coef.append(jnp.where(s < length, weight_ref[s], 0.0))
    total = []
    for j in range(bag):
        c = coef[j]
        for i in range(j):
            c = c + jnp.where(ids[i] == ids[j], coef[i], 0.0)
        total.append(c)
    kept = []
    for j in range(bag):
        c = total[j]
        for k in range(j + 1, bag):
            c = jnp.where(ids[j] == ids[k], 0.0, c)
        kept.append(c)
    largest = functools.reduce(jnp.maximum, kept)
    inverse = 1.0 / largest

    def attempt(k, carry):
        best, scale, factor = carry
        t = 1.0 + k.astype(F32) * (1.0 / tries)
        up = inverse * t
        back = largest * (1.0 / t)
        err = jnp.zeros_like(largest)
        for c in kept:
            miss = (c * up).astype(BF).astype(F32) * back - c
            err = err + miss * miss
        better = err < best
        return (
            jnp.where(better, err, best),
            jnp.where(better, back, scale),
            jnp.where(better, up, factor),
        )

    start = (jnp.full_like(largest, jnp.inf), largest, inverse)
    _, scale, factor = lax.fori_loop(0, tries, attempt, start)
    for s in range(bag):
        slots_ref[s] = ids[s].astype(F32)
        slots_ref[bag + s] = kept[s] * factor
    scale_ref[...] = scale


def bag_slots(ids, weight, length, owners, hot_slots):
    cold = owners * BLOCK
    batch, feats, bag = ids.shape
    slots, scale = pl.pallas_call(
        functools.partial(slots_kernel, cold, hot_slots, 64),
        out_shape=[
            jax.ShapeDtypeStruct((2 * bag, feats, batch), F32),
            jax.ShapeDtypeStruct((feats, batch), F32),
        ],
        name="bag_slots",
    )(jnp.transpose(ids, (2, 1, 0)), jnp.transpose(weight, (2, 1, 0)), length.T)
    return jnp.transpose(slots, (1, 0, 2)), scale


def local(
    emb_table,
    cross_up,
    cross_down,
    cross_bias,
    out_weight,
    bottom_weight,
    bottom_bias,
    dense_in,
    labels,
    lookup_ids,
    bag_weight,
    bag_length,
    want_blocks,
    hot_blocks,
    hot_count,
):
    owners = lax.axis_size(TABLE)
    replicas = lax.axis_size("replica")
    hot_slots = hot_blocks.shape[1]
    _, width = cross_up.shape

    own_hot = own_hot_rows(emb_table, hot_blocks[0], hot_count)
    hot_rows = lax.all_gather(own_hot, TABLE, axis=0, tiled=True)

    wanted = want_blocks.reshape(owners, 1, 1)
    asked_for = lax.all_to_all(wanted, TABLE, split_axis=0, concat_axis=0, tiled=True)
    asked_for = asked_for.reshape(owners)
    served = served_blocks(emb_table, asked_for)
    cold_rows = lax.all_to_all(served, TABLE, split_axis=0, concat_axis=0, tiled=True)
    cold_rows = cold_rows.reshape(-1, EMB)
    cold_count = cold_rows.shape[0]
    hot_total = hot_rows.shape[0]

    slots, scale = bag_slots(lookup_ids, bag_weight, bag_length, owners, hot_slots)
    sel_cold = build_selection(slots, 0, cold_count)
    sel_hot = build_selection(slots, cold_count, hot_total)

    bottom = jax.nn.relu(
        jnp.dot(dense_in, bottom_weight, precision=lax.Precision.HIGHEST) + bottom_bias
    )
    pooled_hot = gather_pooled(hot_rows, sel_hot)
    grads, grad_pooled = cross_layer(
        cold_rows,
        sel_cold,
        pooled_hot,
        scale,
        bottom,
        labels[:, None],
        cross_up,
        cross_down,
        cross_bias[None],
        out_weight[None],
    )

    weights = lax.psum_scatter(grads, TABLE, scatter_dimension=0, tiled=True)

    hot_grad = scatter_rows(sel_hot, grad_pooled, F32)
    hot_mine = lax.psum_scatter(hot_grad, TABLE, scatter_dimension=0, tiled=True)
    cold_grad = scatter_rows(sel_cold, grad_pooled, BF).reshape(owners, BLOCK, EMB)
    returned = lax.all_to_all(cold_grad, TABLE, split_axis=0, concat_axis=0, tiled=True)
    block_grad = collected(
        emb_table.shape[0], asked_for, hot_blocks[0], hot_count, returned, hot_mine
    )

    block_part = block_grad.reshape(replicas, -1, EMB)
    weight_part = weights.astype(BF).reshape(replicas, -1, EMB)
    both = jnp.concatenate([block_part, weight_part], 1)
    both = lax.all_to_all(both, "replica", split_axis=0, concat_axis=0, tiled=True)
    both = both.astype(F32).sum(axis=0)
    table_grad = both[: block_part.shape[1]]
    per = 2 * width // EMB
    mine = both[block_part.shape[1] :][:per].reshape(1, 2 * width)
    up_grad, down_grad = mine[:, :width], mine[:, width:]
    return (up_grad, down_grad, table_grad)


def solution(mesh):
    torus = Mesh(
        mesh.devices.reshape(8, 4, 2, mesh.shape["replica"]),
        ("table_0", "table_1", "table_2", "replica"),
    )
    in_specs = (
        P(TABLE, None),
        P(),
        P(),
        P(),
        P(),
        P(),
        P(),
        P(TABLE_REPLICA, None),
        P(TABLE_REPLICA),
        P(TABLE_REPLICA, None, None),
        P(TABLE_REPLICA, None, None),
        P(TABLE_REPLICA, None),
        P(TABLE, "replica", None, None),
        P(TABLE, None),
        P(TABLE),
    )
    out_specs = (P(TABLE_REPLICA, None), P(TABLE_REPLICA, None), P(TABLE_REPLICA, None))
    return jax.shard_map(local, mesh=torus, in_specs=in_specs, out_specs=out_specs, check_vma=False)
```

time: 399 us -> 450 us (1.13)
  waiting for transfers between devices: 130 us -> 262 us
  other arithmetic: 104 us -> 3.72 us
  Pallas kernels: 0 us -> 97.1 us
  local copies, waits for them, and re-layouts: 93.2 us -> 9.9 us
  starting transfers between devices: 61.3 us -> 5.67 us
  blocking collectives: 0 us -> 55.6 us
  between operations: 1.88 us -> 14.5 us
  matrix products: 7.86 us -> 0.92 us
    reduce_scatter x0 -> x2, waiting for transfers between devices: none -> 257 us  [the longest x1 151 us: local(): weights = lax.psum_scatter(grads, TABLE, scatter_dimension=0, tiled=True)]
    all_to_all x9 -> x0, waiting for transfers between devices: 125 us -> none  [the longest x2 54.3 us: sent_and_summed(): lax.all_to_all(blocks, axis, split_axis=0, concat_axis=0, tiled=True)]
    pallas_call x0 -> x10, Pallas kernels: none -> 97.1 us  [the longest x2 32.4 us: build_selection(): pl.pallas_call(functools.partial(build_kernel, first, tile), grid=(count...]
    scatter-add x1 -> x0, other arithmetic: 80.3 us -> none  [local_step(): cache_grad = jnp.zeros(cached_rows.shape, jnp.float32).at[ids_dev.reshape...]
    all_to_all x0 -> x3, blocking collectives: none -> 55.6 us  [the longest x1 24.6 us: local(): lax.all_to_all(cold_grad, TABLE, split_axis=0, concat_axis=0, tiled=True)]
    all_to_all x9 -> x0, starting transfers between devices: 53.4 us -> none  [the longest x2 16.2 us: sent_to_all(): lax.all_to_all(jnp.broadcast_to(x[None], (devices, *x.shape)), axis, 0, 0...]
    gather x3 -> x0, local copies, waits for them, and re-layouts: 50 us -> none  [the longest x1 47.1 us: local_step(): gathered = cached_rows[ids_dev].astype(jnp.float32)]
    reduce_sum x7 -> x1, other arithmetic: 14.1 us -> 0.04 us  [local(): both = both.astype(F32).sum(axis=0)]
  transfers between devices with their start and end apart: 10 -> 4, of which waited for: 10 -> 3; matrix products, arithmetic and copies ran while one was open for 10% -> 2% of each run, Pallas kernels for 0% -> 14%
where the time goes in v1:
time: 450 us; the launch traced here: 449 us
  waiting for transfers between devices  262 us (58%)
  Pallas kernels  97.1 us (22%)
  blocking collectives  55.6 us (12%)
  between operations  14.5 us (3%)
  local copies, waits for them, and re-layouts  9.9 us (2%)
  starting transfers between devices  5.67 us (1%)
    reduce_scatter x1, waiting for transfers between devices, local(): weights = lax.psum_scatter(grads, TABLE, scatter_dimension=0, tiled=True)  151 us
    reduce_scatter x1, waiting for transfers between devices, local(): lax.psum_scatter(hot_grad, TABLE, scatter_dimension=0, tiled=True)  106 us
    pallas_call x2, Pallas kernels, build_selection(): pl.pallas_call(functools.partial(build_kernel, first, tile), grid=(count...  32.4 us
    all_to_all x1, blocking collectives, local(): lax.all_to_all(cold_grad, TABLE, split_axis=0, concat_axis=0, tiled=True)  24.6 us
    pallas_call x2, Pallas kernels, scatter_rows(): pl.pallas_call(scatter_kernel, grid=(count // tile,), in_specs=[pl.BlockS...  23.2 us
    all_to_all x1, blocking collectives, local(): lax.all_to_all(wanted, TABLE, split_axis=0, concat_axis=0, tiled=True)  20 us
    pallas_call x1, Pallas kernels, cross_layer(): pl.pallas_call(cross_kernel, grid=(count // tile,), in_specs=[pl.BlockSpe...  16.1 us
    pallas_call x1, Pallas kernels, gather_pooled(): pl.pallas_call(gather_kernel, grid=(count // tile,), in_specs=[pl.BlockSp...  14.3 us
  transfers between devices with their start and end apart: 4, of which 3 were waited for; matrix products, arithmetic and copies ran while one was open for 2% of the time, Pallas kernels for 14%

profile of v1, /device:TPU:32, one launch (start us, length us, event | category | flops | bytes accessed | tf_op | source)
XLA Modules:
  0.0 448.9 jit_solution(3972526858088574918)
XLA Ops:
  7.2 0.0 copy-start
  7.2 0.0 copy-start.4
  7.2 0.0 copy-start.5
  7.2 0.0 copy-start.7
  7.2 0.0 copy-start.2
  7.2 0.0 copy-start.3
  7.2 0.0 all-gather.2.cloned.1.call-start
  7.9 2.0 own_hot_rows.1
  9.9 0.0 all-gather.2.cloned.1.call-update
  10.0 0.7 copy.29
  10.7 20.0 %all_to_all.20 = s32[64,1,1]{2,1,0:T(1,128)S(1)} all-to-all(s32[64,1,1]{2,1,0:T(1,128)S(1)} %copy.29), channel_id=1, replica_groups=mesh['table_0'=8,'table_1'=4,'table_2'=2,'replica'=4] {'table_0','table_..., dimensions={0} | all-to-all | bytes 512 | tf_op jit(solution)/shard_map/all_to_all | solution.py:385
  30.7 1.8 reduce.picks_ref
  32.5 1.8 served_blocks.1
  34.4 5.5 %all-to-all-start.1 = ((bf16[64,32,128]{2,1,0:T(8,128)(2,1)}), bf16[64,32,128]{2,1,0:T(8,128)(2,1)S(1)}, u32[]{:S(2)}, u32[]{:S(2)}) async-start(bf16[64,32,128]{2,1,0:T(8,128)(2,1)} %served_blocks.1), calls=%async_computation.1 | async-start | bytes 1048576 | tf_op jit(solution)/shard_map/all_to_all | solution.py:388
  39.9 0.0 reduce-scatter.3.cloned.1.call-start
  40.0 0.6 broadcast_in_dim.11.bias_ref
  40.6 0.6 broadcast_in_dim.12.ow_ref
  41.2 0.7 copy.34.labels_ref
  42.0 0.0 copy-done.2
  42.0 0.6 copy.42
  42.6 0.0 copy-done.3
  42.6 0.6 copy.41
  43.2 5.2 %bag_slots.1 = (f32[8,26,128]{2,1,0:T(8,128)}, f32[26,128]{1,0:T(8,128)}) custom-call(s32[4,26,128]{2,1,0:T(8,128)} %bitcast.32, f32[4,26,128]{2,1,0:T(8,128)} %bitcast.33, s32[26,128]{1,0:T(8,128)} %bitcast.36), custom_call_target="tpu_custom_call" | custom-call | tf_op jit(solution)/shard_map/bag_slots/pallas_call | solution.py:348
  48.4 1.6 copy.40
  50.1 1.4 copy.33
  51.5 0.7 iota.13.iota_ref
  52.2 11.6 %build_selection.2.sel_ref = bf16[2048,3328]{1,0:T(8,128)(2,1)} custom-call(f32[26,8,128]{2,1,0:T(8,128)} %bitcast.29, bf16[256,128]{1,0:T(8,128)(2,1)} %iota.13.iota_ref), custom_call_target="tpu_custom_call" | custom-call | flops 54525952 | bytes 13631488 | tf_op jit(solution)/shard_map/build_selection/pallas_call | solution.py:43
  63.8 20.8 %build_selection.3.sel_ref = bf16[4096,3328]{1,0:T(8,128)(2,1)} custom-call(f32[26,8,128]{2,1,0:T(8,128)} %bitcast.30, bf16[256,128]{1,0:T(8,128)(2,1)} %iota.13.iota_ref), custom_call_target="tpu_custom_call" | custom-call | flops 109051904 | bytes 27262976 | tf_op jit(solution)/shard_map/build_selection/pallas_call | solution.py:43
  84.7 0.9 fusion.bottom_ref
  85.6 3.9 all-gather.2.cloned.1.call-done.rows_ref
  89.5 14.3 %gather_pooled.1.hot_ref = f32[128,3328]{1,0:T(8,128)} custom-call(bf16[4096,128]{1,0:T(8,128)(2,1)} %all-gather.2.cloned.1.call-done.rows_ref, bf16[4096,3328]{1,0:T(8,128)(2,1)} %build_selection.3.sel_ref), custom_call_target="tpu_custom_call" | custom-call | flops 3489660928 | bytes 27262976 | tf_op jit(solution)/shard_map/gather_pooled/pallas_call | solution.py:76
  103.7 0.0 all-to-all-done.1
  103.7 0.8 copy-done.1
  104.6 16.1 %cross_layer.1 = (f32[14336,128]{1,0:T(8,128)}, bf16[3328,128]{1,0:T(8,128)(2,1)}) custom-call(bf16[2048,128]{1,0:T(8,128)(2,1)} %bitcast.26, bf16[2048,3328]{1,0:T(8,128)(2,1)} %build_selection.2.sel_ref, f32[128,3328]{1,0:T(8,128)} %gather_pooled.1.hot_ref, f32[26,128]{1,0:T(8,128)} %get-tuple-element.8.scale_ref, f32[128,26]{1,0:T(8,128)} %bitcast.31, ...), custom_call_target="tpu_custom_call" | custom-call | flops 3103784960 | bytes 20709376 | tf_op jit(solution)/shard_map/cross_layer/pallas_call | solution.py:170
  120.7 15.0 %scatter_rows.3 = f32[4096,128]{1,0:T(8,128)} custom-call(bf16[4096,3328]{1,0:T(8,128)(2,1)} %build_selection.3.sel_ref, bf16[3328,128]{1,0:T(8,128)(2,1)} %get-tuple-element.9.grad_ref), custom_call_target="tpu_custom_call" | custom-call | flops 3489660928 | bytes 27262976 | tf_op jit(solution)/shard_map/scatter_rows/pallas_call | solution.py:213
  135.6 0.0 reduce-scatter.3.cloned.1.call-update
  135.6 0.0 reduce-scatter.5.cloned.1.call-start
  135.7 0.7 reduce-scatter.5.cloned.1.call-update
  136.4 8.3 %scatter_rows.2 = bf16[2048,128]{1,0:T(8,128)(2,1)} custom-call(bf16[2048,3328]{1,0:T(8,128)(2,1)} %build_selection.2.sel_ref, bf16[3328,128]{1,0:T(8,128)(2,1)} %get-tuple-element.9.grad_ref), custom_call_target="tpu_custom_call" | custom-call | flops 1744830464 | bytes 13631488 | tf_op jit(solution)/shard_map/scatter_rows/pallas_call | solution.py:213
  144.7 24.6 %all_to_all.21.back_ref = bf16[64,32,128]{2,1,0:T(8,128)(2,1)} all-to-all(bf16[64,32,128]{2,1,0:T(8,128)(2,1)} %bitcast.27), channel_id=1, replica_groups=mesh['table_0'=8,'table_1'=4,'table_2'=2,'replica'=4] {'table_0','table_..., dimensions={0} | all-to-all | bytes 1048576 | tf_op jit(solution)/shard_map/all_to_all | solution.py:419
  169.2 105.8 %reduce-scatter.3.cloned.1.call-done.hot_ref = f32[64,128]{1,0:T(8,128)} async-done(((f32[4096,128]{1,0:T(8,128)}), f32[64,128]{1,0:T(8,128)}) %reduce-scatter.3.cloned.1.call-update) | async-done | bytes 32784 | tf_op jit(solution)/shard_map/reduce_scatter | solution.py:417
  275.0 2.0 collected.1
  277.0 151.1 %reduce-scatter.5.cloned.1.call-done = f32[224,128]{1,0:T(8,128)} async-done(((f32[14336,128]{1,0:T(8,128)}), f32[224,128]{1,0:T(8,128)}) %reduce-scatter.5.cloned.1.call-update) | async-done | bytes 114704 | tf_op jit(solution)/shard_map/reduce_scatter | solution.py:414
  428.2 0.9 convert_element_type.13
  429.1 1.0 pad_maximum_fusion
  430.0 11.0 %all_to_all.22 = bf16[4,312,128]{2,1,0:T(8,128)(2,1)S(1)} all-to-all(bf16[4,312,128]{2,1,0:T(8,128)(2,1)S(1)} %pad_maximum_fusion), channel_id=1, replica_groups=mesh['table_0'=8,'table_1'=4,'table_2'=2,'replica'=4] {'replica'}, dimensions={0} | all-to-all | bytes 638976 | tf_op jit(solution)/shard_map/all_to_all | solution.py:427
  441.1 0.7 slice.21
  441.8 0.6 fusion.1
  (13 shorter events, 0.1 us)
Async XLA Ops:
  7.2 77.5 %copy-start = (f32[128,13]{0,1:T(8,128)S(1)}, f32[128,13]{0,1:T(8,128)}, u32[]{:S(2)}) copy-start(f32[128,13]{0,1:T(8,128)} %param.22) | copy-start | bytes 19972
  7.2 32.8 %copy-start.4 = (f32[3456]{0:T(1024)S(1)}, f32[3456]{0:T(1024)}, u32[]{:S(2)}) copy-start(f32[3456]{0:T(1024)} %param.18) | copy-start | bytes 41476
  7.2 33.4 %copy-start.5 = (f32[3456]{0:T(1024)S(1)}, f32[3456]{0:T(1024)}, u32[]{:S(2)}) copy-start(f32[3456]{0:T(1024)} %param.19) | copy-start | bytes 41476
  7.2 34.0 %copy-start.7 = (s32[128]{0:T(128)S(1)}, s32[128]{0:T(128)}, u32[]{:S(2)}) copy-start(s32[128]{0:T(128)} %param.23) | copy-start | bytes 1540
  7.2 34.7 %copy-start.2 = (s32[128,26,4]{0,2,1:T(4,128)S(1)}, s32[128,26,4]{0,2,1:T(4,128)}, u32[]{:S(2)}) copy-start(s32[128,26,4]{0,2,1:T(4,128)} %param.24) | copy-start | bytes 159748
  7.2 35.4 %copy-start.3 = (f32[128,26,4]{0,2,1:T(4,128)S(1)}, f32[128,26,4]{0,2,1:T(4,128)}, u32[]{:S(2)}) copy-start(f32[128,26,4]{0,2,1:T(4,128)} %param.25) | copy-start | bytes 159748
  7.2 82.2 %all-gather.2.cloned.1.call-start = ((), (), s32[]{:S(2)}) async-start(), calls=%async_computation.6 | async-start | bytes 1064960 | tf_op jit(solution)/shard_map/all_gather | solution.py:382
  34.4 69.4 %all-to-all-start.1 = ((bf16[64,32,128]{2,1,0:T(8,128)(2,1)}), bf16[64,32,128]{2,1,0:T(8,128)(2,1)S(1)}, u32[]{:S(2)}, u32[]{:S(2)}) async-start(bf16[64,32,128]{2,1,0:T(8,128)(2,1)} %served_blocks.1), calls=%async_computation.1 | async-start | bytes 1048576 | tf_op jit(solution)/shard_map/all_to_all | solution.py:388
  39.9 235.1 %reduce-scatter.3.cloned.1.call-start = ((), (), s32[]{:S(2)}) async-start(), calls=%async_computation.7 | async-start | bytes 2129920 | tf_op jit(solution)/shard_map/reduce_scatter | solution.py:417
  63.8 20.9 %copy-start.6 = (f32[13,128]{1,0:T(8,128)S(1)}, f32[13,128]{1,0:T(8,128)}, u32[]{:S(2)}) copy-start(f32[13,128]{1,0:T(8,128)} %param.20) | copy-start | bytes 19972
  63.8 20.9 %copy-start.8 = (f32[128]{0:T(128)S(1)}, f32[128]{0:T(128)}, u32[]{:S(2)}) copy-start(f32[128]{0:T(128)} %param.21) | copy-start | bytes 1540
  103.7 0.8 copy-start.1
  135.6 292.5 %reduce-scatter.5.cloned.1.call-start = ((), (), s32[]{:S(2)}) async-start(), calls=%async_computation.8 | async-start | bytes 7454720 | tf_op jit(solution)/shard_map/reduce_scatter | solution.py:414
Sparse Core Ops, SparseCore 0:
  10.8 78.6 all-gather.1
  135.8 139.1 reduce-scatter.2
  279.2 148.8 reduce-scatter.4

commit v2 on v1

--- a/solution.py
+++ b/solution.py
@@ -11,6 +11,8 @@
 EMB = 128
 BLOCK = 32
 TABLE = ("table_0", "table_1", "table_2")
+FAR = "table_0"
+NEAR = ("table_1", "table_2", "replica")
 TABLE_REPLICA = ("table_0", "table_1", "table_2", "replica")
 BF = jnp.bfloat16
 F32 = jnp.float32
@@ -56,43 +58,10 @@
     )(slots, iota)
 
 
-def gather_kernel(rows_ref, sel_ref, out_ref):
-    part = lax.dot_general(
-        rows_ref[...], sel_ref[...], (((0,), (0,)), ((), ())), preferred_element_type=F32
-    )
-
-    @pl.when(pl.program_id(0) == 0)
-    def _():
-        out_ref[...] = part
-
-    @pl.when(pl.program_id(0) > 0)
-    def _():
-        out_ref[...] += part
-
-
-def gather_pooled(rows, sel):
-    tile = 512
-    count, bags = sel.shape
-    return pl.pallas_call(
-        gather_kernel,
-        grid=(count // tile,),
-        in_specs=[
-            pl.BlockSpec((tile, EMB), lambda i: (i, 0)),
-            pl.BlockSpec((tile, bags), lambda i: (i, 0)),
-        ],
-        out_specs=pl.BlockSpec((EMB, bags), lambda i: (0, 0)),
-        out_shape=jax.ShapeDtypeStruct((EMB, bags), F32),
-        cost_estimate=pl.CostEstimate(
-            flops=2 * count * bags * EMB, bytes_accessed=count * bags * 2, transcendentals=0
-        ),
-        name="gather_pooled",
-    )(rows, sel)
-
-
 def cross_kernel(
+    near,
     rows_ref,
     sel_ref,
-    hot_ref,
     scale_ref,
     scale_t_ref,
     bottom_ref,
@@ -101,10 +70,11 @@
     down_ref,
     bias_ref,
     ow_ref,
-    lines_ref,
+    grads_ref,
     gpool_ref,
     acc,
     base_ref,
+    lines_ref,
 ):
     step = pl.program_id(0)
     part = lax.dot_general(
@@ -113,7 +83,7 @@
 
     @pl.when(step == 0)
     def _():
-        acc[...] = hot_ref[...] + part
+        acc[...] = part
 
     @pl.when(step > 0)
     def _():
@@ -145,13 +115,18 @@
         down_part = lax.dot_general(g_low, base, tn, preferred_element_type=F32)
         rank, per = up_part.shape[0], feats + 1
         lines = lines_ref.shape[0] // rank
-        for c in range(per):
-            lines_ref[pl.ds(c, rank, stride=lines), :] = up_part[:, c * EMB : (c + 1) * EMB]
-            lines_ref[pl.ds(per + c, rank, stride=lines), :] = down_part[
-                :, c * EMB : (c + 1) * EMB
-            ]
-        for c in range(2 * per, lines):
-            lines_ref[pl.ds(c, rank, stride=lines), :] = jnp.zeros((rank, EMB), F32)
+        far = rank // near
+        for z in range(far):
+            part_rows = slice(z * near, (z + 1) * near)
+            for c in range(lines):
+                if c < per:
+                    part = up_part[part_rows, c * EMB : (c + 1) * EMB]
+                elif c < 2 * per:
+                    part = down_part[part_rows, (c - per) * EMB : (c - per + 1) * EMB]
+                else:
+                    part = jnp.zeros((near, EMB), F32)
+                lines_ref[pl.ds(z * lines + c, near, stride=far * lines), :] = part
+        grads_ref[...] = lines_ref[...].astype(BF)
         grad_base = grad_crossed * (gate + 1.0) + jnp.dot(
             g_low, down_ref[...], preferred_element_type=F32
         )
@@ -160,7 +135,7 @@
             gpool_ref[f * batch : (f + 1) * batch, :] = block.astype(BF)
 
 
-def cross_layer(rows, sel, pooled_hot, scale, bottom, labels, up, down, bias, ow):
+def cross_layer(near, rows, sel, scale, bottom, labels, up, down, bias, ow):
     tile = 512
     count, bags = sel.shape
     rank, width = up.shape
@@ -168,12 +143,11 @@
     lines = rank * pl.cdiv(2 * width // EMB, 8) * 8
     whole = lambda *shape: pl.BlockSpec(shape, lambda i: (0,) * len(shape))
     return pl.pallas_call(
-        cross_kernel,
+        functools.partial(cross_kernel, near),
         grid=(count // tile,),
         in_specs=[
             pl.BlockSpec((tile, EMB), lambda i: (i, 0)),
             pl.BlockSpec((tile, bags), lambda i: (i, 0)),
-            whole(EMB, bags),
             whole(*scale.shape),
             whole(batch, scale.shape[0]),
             whole(batch, EMB),
@@ -185,12 +159,13 @@
         ],
         out_specs=[whole(lines, EMB), whole(bags, EMB)],
         out_shape=[
-            jax.ShapeDtypeStruct((lines, EMB), F32),
+            jax.ShapeDtypeStruct((lines, EMB), BF),
             jax.ShapeDtypeStruct((bags, EMB), BF),
         ],
         scratch_shapes=[
             pltpu.VMEM((EMB, bags), F32),
             pltpu.VMEM((batch, width), BF),
+            pltpu.VMEM((lines, EMB), F32),
         ],
         cost_estimate=pl.CostEstimate(
             flops=2 * count * bags * EMB + 12 * batch * rank * width,
@@ -198,7 +173,7 @@
             transcendentals=batch,
         ),
         name="cross_layer",
-    )(rows, sel, pooled_hot, scale, scale.T, bottom, labels, up, down, bias, ow)
+    )(rows, sel, scale, scale.T, bottom, labels, up, down, bias, ow)
 
 
 def scatter_kernel(sel_ref, grad_ref, out_ref):
@@ -226,68 +201,63 @@
     )(sel, grad)
 
 
-def hot_kernel(count_ref, picks_ref, block_ref, out_ref):
-    live = pl.program_id(0) < count_ref[0]
-    rows = block_ref[...]
-    out_ref[...] = jnp.where(live, rows, jnp.zeros_like(rows))
-
-
-def own_hot_rows(emb_table, picks, count):
-    slots = picks.shape[0]
-    return pl.pallas_call(
-        hot_kernel,
-        grid_spec=pltpu.PrefetchScalarGridSpec(
-            num_scalar_prefetch=2,
-            grid=(slots,),
-            in_specs=[pl.BlockSpec((BLOCK, EMB), lambda s, count, picks: (picks[s], 0))],
-            out_specs=pl.BlockSpec((BLOCK, EMB), lambda s, count, picks: (s, 0)),
-        ),
-        out_shape=jax.ShapeDtypeStruct((slots * BLOCK, EMB), BF),
-        name="own_hot_rows",
-    )(count, picks, emb_table)
-
-
-def serve_kernel(picks_ref, table_ref, out_ref):
+def serve_kernel(picks_ref, hot_picks_ref, count_ref, table_ref, out_ref):
+    hot = []
+    for s in range(hot_picks_ref.shape[0]):
+        start = pl.multiple_of(hot_picks_ref[s] * BLOCK, BLOCK)
+        rows = table_ref[pl.ds(start, BLOCK), :]
+        hot.append(jnp.where(s < count_ref[0], rows, jnp.zeros_like(rows)))
     for i in range(out_ref.shape[0]):
         start = pl.multiple_of(picks_ref[i] * BLOCK, BLOCK)
-        out_ref[i] = table_ref[pl.ds(start, BLOCK), :]
-
-
-def served_blocks(emb_table, picks):
-    owners = picks.shape[0]
+        out_ref[i, :BLOCK, :] = table_ref[pl.ds(start, BLOCK), :]
+        for s, rows in enumerate(hot):
+            out_ref[i, (s + 1) * BLOCK : (s + 2) * BLOCK, :] = rows
+
+
+def served_rows(emb_table, picks, hot_picks, count):
+    smem = pl.BlockSpec(memory_space=pltpu.SMEM)
+    vmem = pl.BlockSpec(memory_space=pltpu.VMEM)
+    share = (1 + hot_picks.shape[0]) * BLOCK
     return pl.pallas_call(
         serve_kernel,
-        in_specs=[
-            pl.BlockSpec(memory_space=pltpu.SMEM),
-            pl.BlockSpec(memory_space=pltpu.VMEM),
-        ],
-        out_shape=jax.ShapeDtypeStruct((owners, BLOCK, EMB), BF),
-        name="served_blocks",
-    )(picks, emb_table)
-
-
-def collect_kernel(picks_ref, hot_picks_ref, count_ref, back_ref, hot_ref, out_ref, acc):
+        in_specs=[smem, smem, smem, vmem],
+        out_shape=jax.ShapeDtypeStruct((picks.shape[0], share, EMB), BF),
+        name="served_rows",
+    )(picks, hot_picks, count, emb_table)
+
+
+def collect_kernel(picks_ref, hot_picks_ref, count_ref, me_ref, back_ref, own_ref, *others):
+    *send_refs, acc = others
     acc[...] = jnp.zeros_like(acc)
-    for i in range(back_ref.shape[0]):
+    peers, share, _ = back_ref.shape
+    hot = jnp.zeros((share - BLOCK, EMB), F32)
+    for i in range(peers):
         start = pl.multiple_of(picks_ref[i] * BLOCK, BLOCK)
-        acc[pl.ds(start, BLOCK), :] += back_ref[i].astype(F32)
+        acc[pl.ds(start, BLOCK), :] += back_ref[i, :BLOCK, :].astype(F32)
+        hot = hot + back_ref[i, BLOCK:, :].astype(F32)
     for s in range(hot_picks_ref.shape[0]):
         start = pl.multiple_of(hot_picks_ref[s] * BLOCK, BLOCK)
-        hot = hot_ref[s * BLOCK : (s + 1) * BLOCK, :]
-        acc[pl.ds(start, BLOCK), :] += jnp.where(s < count_ref[0], hot, jnp.zeros_like(hot))
-    out_ref[...] = acc[...].astype(out_ref.dtype)
-
-
-def collected(rows, picks, hot_picks, count, back, hot):
+        rows = hot[s * BLOCK : (s + 1) * BLOCK]
+        acc[pl.ds(start, BLOCK), :] += jnp.where(s < count_ref[0], rows, jnp.zeros_like(rows))
+    part, parts = own_ref.shape[0], len(send_refs) + 1
+    for k, ref in enumerate((own_ref, *send_refs)):
+        whose = lax.rem(me_ref[0] + k, parts)
+        start = pl.multiple_of(whose * part, part)
+        ref[...] = acc[pl.ds(start, part), :].astype(ref.dtype)
+
+
+def collected(rows, parts, picks, hot_picks, count, me, back):
     smem = pl.BlockSpec(memory_space=pltpu.SMEM)
     vmem = pl.BlockSpec(memory_space=pltpu.VMEM)
     return pl.pallas_call(
         collect_kernel,
-        in_specs=[smem, smem, smem, vmem, vmem],
-        out_shape=jax.ShapeDtypeStruct((rows, EMB), BF),
+        in_specs=[smem, smem, smem, smem, vmem],
+        out_shape=[
+            jax.ShapeDtypeStruct((rows // parts, EMB), BF if k else F32) for k in range(parts)
+        ],
         scratch_shapes=[pltpu.VMEM((rows, EMB), F32)],
         name="collected",
-    )(picks, hot_picks, count, back, hot)
+    )(picks, hot_picks, count, me, back)
 
 
 def slots_kernel(cold, hot_slots, tries, ids_ref, weight_ref, length_ref, slots_ref, scale_ref):
@@ -298,10 +268,9 @@
     ids, coef = [], []
     for s in range(bag):
         i = ids_ref[s]
-        h = i - cold
-        slot, rest = h >> cold_bits, h & (cold - 1)
-        moved = cold + ((rest >> row_bits) * hot_slots + slot) * BLOCK + (rest & (BLOCK - 1))
-        ids.append(jnp.where(i < cold, i, moved))
+        slot, rest = i >> cold_bits, i & (cold - 1)
+        owner, row = rest >> row_bits, rest & (BLOCK - 1)
+        ids.append((owner * (1 + hot_slots) + slot) * BLOCK + row)
         coef.append(jnp.where(s < length, weight_ref[s], 0.0))
     total = []
     for j in range(bag):
@@ -376,32 +345,28 @@
     owners = lax.axis_size(TABLE)
     replicas = lax.axis_size("replica")
     hot_slots = hot_blocks.shape[1]
-    _, width = cross_up.shape
-
-    own_hot = own_hot_rows(emb_table, hot_blocks[0], hot_count)
-    hot_rows = lax.all_gather(own_hot, TABLE, axis=0, tiled=True)
+    rank, width = cross_up.shape
 
     wanted = want_blocks.reshape(owners, 1, 1)
     asked_for = lax.all_to_all(wanted, TABLE, split_axis=0, concat_axis=0, tiled=True)
     asked_for = asked_for.reshape(owners)
-    served = served_blocks(emb_table, asked_for)
-    cold_rows = lax.all_to_all(served, TABLE, split_axis=0, concat_axis=0, tiled=True)
-    cold_rows = cold_rows.reshape(-1, EMB)
-    cold_count = cold_rows.shape[0]
-    hot_total = hot_rows.shape[0]
+    served = served_rows(emb_table, asked_for, hot_blocks[0], hot_count)
+    fetched = lax.all_to_all(served, TABLE, split_axis=0, concat_axis=0, tiled=True)
+    shares = fetched.shape
+    fetched = fetched.reshape(-1, EMB)
 
     slots, scale = bag_slots(lookup_ids, bag_weight, bag_length, owners, hot_slots)
-    sel_cold = build_selection(slots, 0, cold_count)
-    sel_hot = build_selection(slots, cold_count, hot_total)
+    sel = build_selection(slots, 0, fetched.shape[0])
 
     bottom = jax.nn.relu(
         jnp.dot(dense_in, bottom_weight, precision=lax.Precision.HIGHEST) + bottom_bias
     )
-    pooled_hot = gather_pooled(hot_rows, sel_hot)
+    far = lax.axis_size(FAR)
+    near = lax.axis_size(NEAR)
     grads, grad_pooled = cross_layer(
-        cold_rows,
-        sel_cold,
-        pooled_hot,
+        near,
+        fetched,
+        sel,
         scale,
         bottom,
         labels[:, None],
@@ -411,24 +376,32 @@
         out_weight[None],
     )
 
-    weights = lax.psum_scatter(grads, TABLE, scatter_dimension=0, tiled=True)
-
-    hot_grad = scatter_rows(sel_hot, grad_pooled, F32)
-    hot_mine = lax.psum_scatter(hot_grad, TABLE, scatter_dimension=0, tiled=True)
-    cold_grad = scatter_rows(sel_cold, grad_pooled, BF).reshape(owners, BLOCK, EMB)
-    returned = lax.all_to_all(cold_grad, TABLE, split_axis=0, concat_axis=0, tiled=True)
-    block_grad = collected(
-        emb_table.shape[0], asked_for, hot_blocks[0], hot_count, returned, hot_mine
-    )
-
-    block_part = block_grad.reshape(replicas, -1, EMB)
-    weight_part = weights.astype(BF).reshape(replicas, -1, EMB)
-    both = jnp.concatenate([block_part, weight_part], 1)
-    both = lax.all_to_all(both, "replica", split_axis=0, concat_axis=0, tiled=True)
-    both = both.astype(F32).sum(axis=0)
-    table_grad = both[: block_part.shape[1]]
+    parts = lax.all_to_all(
+        grads.reshape(near, -1, EMB), NEAR, split_axis=0, concat_axis=0, tiled=True
+    )
+
+    row_grad = scatter_rows(sel, grad_pooled, BF).reshape(shares)
+    row_grad, parts = lax.optimization_barrier((row_grad, parts))
+    returned = lax.all_to_all(row_grad, TABLE, split_axis=0, concat_axis=0, tiled=True)
+    nearer = parts.astype(F32).sum(axis=0).astype(BF).reshape(far, -1, EMB)
+    nearer, returned = lax.optimization_barrier((nearer, returned))
+    own, *sends = collected(
+        emb_table.shape[0],
+        replicas,
+        asked_for,
+        hot_blocks[0],
+        hot_count,
+        lax.axis_index("replica").reshape(1),
+        returned,
+    )
+    table_grad = own
+    for k, part in enumerate(sends, 1):
+        ring = [(i, (i + k) % replicas) for i in range(replicas)]
+        table_grad = table_grad + lax.ppermute(part, "replica", ring).astype(F32)
+
+    mine = lax.all_to_all(nearer, FAR, split_axis=0, concat_axis=0, tiled=True)
     per = 2 * width // EMB
-    mine = both[block_part.shape[1] :][:per].reshape(1, 2 * width)
+    mine = mine.astype(F32).sum(axis=0)[:per].reshape(rank // (near * far), 2 * width)
     up_grad, down_grad = mine[:, :width], mine[:, width:]
     return (up_grad, down_grad, table_grad)
 

time: 450 us -> 233 us (0.52)
  waiting for transfers between devices: 262 us -> 74.1 us
  blocking collectives: 55.6 us -> 0 us
  starting transfers between devices: 5.67 us -> 43.4 us
  between operations: 14.5 us -> 1.4 us
  Pallas kernels: 97.1 us -> 92.4 us
    reduce_scatter x2 -> x0, waiting for transfers between devices: 257 us -> none  [the longest x1 151 us: local(): weights = lax.psum_scatter(grads, TABLE, scatter_dimension=0, tiled=True)]
    all_to_all x0 -> x4, waiting for transfers between devices: none -> 74.1 us  [the longest x1 35.9 us: local(): lax.all_to_all(row_grad, TABLE, split_axis=0, concat_axis=0, tiled=True)]
    all_to_all x3 -> x0, blocking collectives: 55.6 us -> none  [the longest x1 24.6 us: local(): lax.all_to_all(cold_grad, TABLE, split_axis=0, concat_axis=0, tiled=True)]
    all_to_all x0 -> x4, starting transfers between devices: none -> 33.1 us  [the longest x1 11.6 us: local(): lax.all_to_all(wanted, TABLE, split_axis=0, concat_axis=0, tiled=True)]
    ppermute x0 -> x3, starting transfers between devices: none -> 4.55 us  [local(): table_grad = table_grad + lax.ppermute(part, 'replica', ring).astype(F32)]
    pallas_call x2 -> x1, Pallas kernels: 32.4 us -> 30.3 us  [build_selection(): pl.pallas_call(functools.partial(build_kernel, first, tile), grid=(count...]
    pallas_call x2 -> x1, Pallas kernels: 23.2 us -> 21.2 us  [scatter_rows(): pl.pallas_call(scatter_kernel, grid=(count // tile,), in_specs=[pl.BlockS...]
    pallas_call x5 -> x3, Pallas kernels: 36.2 us -> 35.7 us  [the longest x1 30.8 us: cross_layer(): pl.pallas_call(functools.partial(cross_kernel, near), grid=(count // tile...]
  transfers between devices with their start and end apart: 4 -> 8, of which waited for: 3 -> 4; matrix products, arithmetic and copies ran while one was open for 2% -> 6% of each run, Pallas kernels for 14% -> 25%
where the time goes in v2:
time: 233 us; the launch traced here: 230 us
  Pallas kernels  92.4 us (40%)
  waiting for transfers between devices  74.1 us (32%)
  starting transfers between devices  43.4 us (19%)
  local copies, waits for them, and re-layouts  11.4 us (5%)
  other arithmetic  6.65 us (3%)
    all_to_all x1, waiting for transfers between devices, local(): lax.all_to_all(row_grad, TABLE, split_axis=0, concat_axis=0, tiled=True)  35.9 us
    pallas_call x1, Pallas kernels, cross_layer(): pl.pallas_call(functools.partial(cross_kernel, near), grid=(count // tile...  30.8 us
    pallas_call x1, Pallas kernels, build_selection(): pl.pallas_call(functools.partial(build_kernel, first, tile), grid=(count...  30.3 us
    all_to_all x1, waiting for transfers between devices, local(): lax.all_to_all(grads.reshape(near, -1, EMB), NEAR, split_axis=0, concat_a...  24.4 us
    pallas_call x1, Pallas kernels, scatter_rows(): pl.pallas_call(scatter_kernel, grid=(count // tile,), in_specs=[pl.BlockS...  21.2 us
    all_to_all x1, starting transfers between devices, local(): lax.all_to_all(wanted, TABLE, split_axis=0, concat_axis=0, tiled=True)  11.6 us
    all_to_all x1, starting transfers between devices, local(): lax.all_to_all(row_grad, TABLE, split_axis=0, concat_axis=0, tiled=True)  9.42 us
    all_to_all x1, waiting for transfers between devices, local(): lax.all_to_all(wanted, TABLE, split_axis=0, concat_axis=0, tiled=True)  7.93 us
  transfers between devices with their start and end apart: 8, of which 4 were waited for; matrix products, arithmetic and copies ran while one was open for 6% of the time, Pallas kernels for 25%

profile of v2, /device:TPU:32, one launch (start us, length us, event | category | flops | bytes accessed | tf_op | source)
XLA Modules:
  0.0 230.3 jit_solution(9658991976749496399)
XLA Ops:
  0.6 0.0 copy-start
  0.6 1.4 copy.38
  2.0 11.6 %all-to-all-start = ((s32[64,1,1]{2,1,0:T(1,128)}), s32[64,1,1]{2,1,0:T(1,128)S(1)}, u32[]{:S(2)}, u32[]{:S(2)}) async-start(s32[64,1,1]{2,1,0:T(1,128)} %copy.38), calls=%async_computation | async-start | bytes 65536 | tf_op jit(solution)/shard_map/all_to_all | solution.py:351
  14.3 7.9 %all-to-all-done = s32[64,1,1]{2,1,0:T(1,128)S(1)} async-done(((s32[64,1,1]{2,1,0:T(1,128)}), s32[64,1,1]{2,1,0:T(1,128)S(1)}, u32[]{:S(2)}, u32[]{:S(2)}) %all-to-all-start) | async-done | bytes 288 | tf_op jit(solution)/shard_map/all_to_all | solution.py:351
  22.2 1.8 reduce.1.picks_ref
  24.0 2.3 %served_rows.1 = bf16[64,96,128]{2,1,0:T(8,128)(2,1)} custom-call(s32[64]{0:T(128)} %reduce.1.picks_ref, s32[2]{0:T(128)} %bitcast.36, s32[1]{0:T(128)S(6)} %copy.50.count_ref, bf16[1024,128]{1,0:T(8,128)(2,1)} %table_ref.1), custom_call_target="tpu_custom_call" | custom-call | tf_op jit(solution)/shard_map/served_rows/pallas_call | solution.py:221
  26.3 0.0 copy-start.6
  26.4 5.7 %all-to-all-start.1 = ((bf16[64,96,128]{2,1,0:T(8,128)(2,1)}), bf16[64,96,128]{2,1,0:T(8,128)(2,1)S(1)}, u32[]{:S(2)}, u32[]{:S(2)}) async-start(bf16[64,96,128]{2,1,0:T(8,128)(2,1)} %served_rows.1), calls=%async_computation.1 | async-start | bytes 3145728 | tf_op jit(solution)/shard_map/all_to_all | solution.py:354
  32.1 0.0 copy-done.3
  32.1 0.6 copy.47
  32.7 0.0 copy-done.4
  32.7 0.6 copy.48
  33.4 5.2 %bag_slots.1 = (f32[8,26,128]{2,1,0:T(8,128)}, f32[26,128]{1,0:T(8,128)}) custom-call(s32[4,26,128]{2,1,0:T(8,128)} %bitcast.33, f32[4,26,128]{2,1,0:T(8,128)} %bitcast.32, s32[26,128]{1,0:T(8,128)} %bitcast.35), custom_call_target="tpu_custom_call" | custom-call | tf_op jit(solution)/shard_map/bag_slots/pallas_call | solution.py:317
  38.6 1.6 copy.46
  40.2 1.4 copy.39
  41.7 0.0 copy-done.8
  41.7 0.7 copy.40.labels_ref
  42.4 0.0 copy-done.5
  42.4 0.6 broadcast_in_dim.11.bias_ref
  43.0 0.0 copy-done.6
  43.0 0.6 broadcast_in_dim.12.ow_ref
  43.6 0.7 iota.7.iota_ref
  44.4 30.3 %build_selection.1.sel_ref = bf16[6144,3328]{1,0:T(8,128)(2,1)} custom-call(f32[26,8,128]{2,1,0:T(8,128)} %bitcast.30, bf16[256,128]{1,0:T(8,128)(2,1)} %iota.7.iota_ref), custom_call_target="tpu_custom_call" | custom-call | flops 163577856 | bytes 40894464 | tf_op jit(solution)/shard_map/build_selection/pallas_call | solution.py:45
  74.7 0.0 copy-done
  74.7 0.0 copy-done.7
  74.7 0.0 copy-done.9
  74.7 0.9 fusion.bottom_ref
  75.7 0.0 all-to-all-done.1
  75.7 1.1 copy-done.1
  76.8 30.8 %cross_layer.1 = (bf16[14336,128]{1,0:T(8,128)(2,1)}, bf16[3328,128]{1,0:T(8,128)(2,1)}) custom-call(bf16[6144,128]{1,0:T(8,128)(2,1)} %bitcast.27, bf16[6144,3328]{1,0:T(8,128)(2,1)} %build_selection.1.sel_ref, f32[26,128]{1,0:T(8,128)} %get-tuple-element.16.scale_ref, f32[128,26]{1,0:T(8,128)} %bitcast.31, f32[128,128]{1,0:T(8,128)} %fusion.bottom_ref, ...), custom_call_target="tpu_custom_call" | custom-call | flops 6593445888 | bytes 47972352 | tf_op jit(solution)/shard_map/cross_layer/pallas_call | solution.py:145
  107.6 7.4 %all-to-all-start.2 = ((bf16[32,448,128]{2,1,0:T(8,128)(2,1)}), bf16[32,448,128]{2,1,0:T(8,128)(2,1)}, u32[]{:S(2)}, u32[]{:S(2)}) async-start(bf16[32,448,128]{2,1,0:T(8,128)(2,1)} %bitcast.29), calls=%async_computation.2 | async-start | bytes 7340032 | tf_op jit(solution)/shard_map/all_to_all | solution.py:379
  115.0 21.2 %scatter_rows.1 = bf16[6144,128]{1,0:T(8,128)(2,1)} custom-call(bf16[6144,3328]{1,0:T(8,128)(2,1)} %build_selection.1.sel_ref, bf16[3328,128]{1,0:T(8,128)(2,1)} %get-tuple-element.17.grad_ref), custom_call_target="tpu_custom_call" | custom-call | flops 5234491392 | bytes 40894464 | tf_op jit(solution)/shard_map/scatter_rows/pallas_call | solution.py:188
  136.2 24.4 %all-to-all-done.2 = bf16[32,448,128]{2,1,0:T(8,128)(2,1)} async-done(((bf16[32,448,128]{2,1,0:T(8,128)(2,1)}), bf16[32,448,128]{2,1,0:T(8,128)(2,1)}, u32[]{:S(2)}, u32[]{:S(2)}) %all-to-all-start.2) | async-done | bytes 3670048 | tf_op jit(solution)/shard_map/all_to_all | solution.py:379
  160.6 9.4 %all-to-all-start.3 = ((bf16[64,96,128]{2,1,0:T(8,128)(2,1)}), bf16[64,96,128]{2,1,0:T(8,128)(2,1)S(1)}, u32[]{:S(2)}, u32[]{:S(2)}) async-start(bf16[64,96,128]{2,1,0:T(8,128)(2,1)} %bitcast.28), calls=%async_computation.3 | async-start | bytes 3145728 | tf_op jit(solution)/shard_map/all_to_all | solution.py:385
  170.0 3.2 %reduce_sum.21 = bf16[448,128]{1,0:T(8,128)(2,1)} reduce(bf16[32,448,128]{2,1,0:T(8,128)(2,1)} %all-to-all-done.2, bf16[]{:T(256)} %constant.8.clone.1), dimensions={0}, to_apply=%region_0.1 | reduce | flops 1777664 | bytes 3784706 | tf_op jit(solution)/shard_map/reduce_sum | solution.py:386
  173.2 35.9 %all-to-all-done.3.back_ref = bf16[64,96,128]{2,1,0:T(8,128)(2,1)S(1)} async-done(((bf16[64,96,128]{2,1,0:T(8,128)(2,1)}), bf16[64,96,128]{2,1,0:T(8,128)(2,1)S(1)}, u32[]{:S(2)}, u32[]{:S(2)}) %all-to-all-start.3) | async-done | bytes 1572896 | tf_op jit(solution)/shard_map/all_to_all | solution.py:385
  209.2 1.2 copy-done.2
  210.3 2.6 %collected.1 = (f32[256,128]{1,0:T(8,128)}, bf16[256,128]{1,0:T(8,128)(2,1)}, bf16[256,128]{1,0:T(8,128)(2,1)}, bf16[256,128]{1,0:T(8,128)(2,1)}) custom-call(s32[64]{0:T(128)} %reduce.1.picks_ref, s32[2]{0:T(128)} %bitcast.37, s32[1]{0:T(128)S(6)} %copy.50.count_ref, s32[1]{0:T(128)} %bitcast.12.me_ref, bf16[64,96,128]{2,1,0:T(8,128)(2,1)} %copy-done.2), custom_call_target="tpu_custom_call" | custom-call | tf_op jit(solution)/shard_map/collected/pallas_call | solution.py:252
  212.9 0.5 collective-permute-start
  213.4 4.0 %collective-permute-start.1 = (bf16[256,128]{1,0:T(8,128)(2,1)}, bf16[256,128]{1,0:T(8,128)(2,1)S(1)}, u32[]{:S(2)}, u32[]{:S(2)}) collective-permute-start(bf16[256,128]{1,0:T(8,128)(2,1)} %get-tuple-element.25), channel_id=1, source_target_pairs={{0,2},{1,3},{2,0},{3,1},{4,6},{5,7},{6,4},{7,5},{8,10},{9,11},{10,... | collective-permute-start | bytes 196616 | tf_op jit(solution)/shard_map/ppermute | solution.py:400
  217.4 0.0 collective-permute-start.2
  217.4 4.7 %all-to-all-start.4 = ((bf16[8,56,128]{2,1,0:T(8,128)(2,1)}), bf16[8,56,128]{2,1,0:T(8,128)(2,1)S(1)}, u32[]{:S(2)}, u32[]{:S(2)}) async-start(bf16[8,56,128]{2,1,0:T(8,128)(2,1)} %bitcast.11), calls=%async_computation.4 | async-start | bytes 229376 | tf_op jit(solution)/shard_map/all_to_all | solution.py:402
  222.2 0.0 collective-permute-done
  222.2 0.0 collective-permute-done.1
  222.2 0.0 collective-permute-done.2
  222.2 1.6 convert_add_fusion
  223.8 5.8 %all-to-all-done.4 = bf16[8,56,128]{2,1,0:T(8,128)(2,1)S(1)} async-done(((bf16[8,56,128]{2,1,0:T(8,128)(2,1)}), bf16[8,56,128]{2,1,0:T(8,128)(2,1)S(1)}, u32[]{:S(2)}, u32[]{:S(2)}) %all-to-all-start.4) | async-done | bytes 114720 | tf_op jit(solution)/shard_map/all_to_all | solution.py:402
  229.7 0.6 fusion.1
  (12 shorter events, 0.1 us)
Async XLA Ops:
  0.6 74.1 %copy-start = (f32[128,13]{0,1:T(8,128)S(1)}, f32[128,13]{0,1:T(8,128)}, u32[]{:S(2)}) copy-start(f32[128,13]{0,1:T(8,128)} %param.22) | copy-start | bytes 19972
  2.0 20.2 %all-to-all-start = ((s32[64,1,1]{2,1,0:T(1,128)}), s32[64,1,1]{2,1,0:T(1,128)S(1)}, u32[]{:S(2)}, u32[]{:S(2)}) async-start(s32[64,1,1]{2,1,0:T(1,128)} %copy.38), calls=%async_computation | async-start | bytes 65536 | tf_op jit(solution)/shard_map/all_to_all | solution.py:351
  26.3 5.8 %copy-start.3 = (f32[128,26,4]{0,2,1:T(4,128)S(1)}, f32[128,26,4]{0,2,1:T(4,128)}, u32[]{:S(2)}) copy-start(f32[128,26,4]{0,2,1:T(4,128)} %param.25) | copy-start | bytes 159748
  26.3 6.4 %copy-start.4 = (s32[128,26,4]{0,2,1:T(4,128)S(1)}, s32[128,26,4]{0,2,1:T(4,128)}, u32[]{:S(2)}) copy-start(s32[128,26,4]{0,2,1:T(4,128)} %param.24) | copy-start | bytes 159748
  26.3 15.3 %copy-start.8 = (s32[128]{0:T(128)S(1)}, s32[128]{0:T(128)}, u32[]{:S(2)}) copy-start(s32[128]{0:T(128)} %param.23) | copy-start | bytes 1540
  26.3 16.1 %copy-start.5 = (f32[3456]{0:T(1024)S(1)}, f32[3456]{0:T(1024)}, u32[]{:S(2)}) copy-start(f32[3456]{0:T(1024)} %param.18) | copy-start | bytes 41476
  26.3 16.7 %copy-start.6 = (f32[3456]{0:T(1024)S(1)}, f32[3456]{0:T(1024)}, u32[]{:S(2)}) copy-start(f32[3456]{0:T(1024)} %param.19) | copy-start | bytes 41476
  26.4 49.3 %all-to-all-start.1 = ((bf16[64,96,128]{2,1,0:T(8,128)(2,1)}), bf16[64,96,128]{2,1,0:T(8,128)(2,1)S(1)}, u32[]{:S(2)}, u32[]{:S(2)}) async-start(bf16[64,96,128]{2,1,0:T(8,128)(2,1)} %served_rows.1), calls=%async_computation.1 | async-start | bytes 3145728 | tf_op jit(solution)/shard_map/all_to_all | solution.py:354
  44.4 30.4 %copy-start.7 = (f32[13,128]{1,0:T(8,128)S(1)}, f32[13,128]{1,0:T(8,128)}, u32[]{:S(2)}) copy-start(f32[13,128]{1,0:T(8,128)} %param.20) | copy-start | bytes 19972
  44.4 30.4 %copy-start.9 = (f32[128]{0:T(128)S(1)}, f32[128]{0:T(128)}, u32[]{:S(2)}) copy-start(f32[128]{0:T(128)} %param.21) | copy-start | bytes 1540
  75.7 1.1 copy-start.1
  107.6 53.0 %all-to-all-start.2 = ((bf16[32,448,128]{2,1,0:T(8,128)(2,1)}), bf16[32,448,128]{2,1,0:T(8,128)(2,1)}, u32[]{:S(2)}, u32[]{:S(2)}) async-start(bf16[32,448,128]{2,1,0:T(8,128)(2,1)} %bitcast.29), calls=%async_computation.2 | async-start | bytes 7340032 | tf_op jit(solution)/shard_map/all_to_all | solution.py:379
  160.6 48.6 %all-to-all-start.3 = ((bf16[64,96,128]{2,1,0:T(8,128)(2,1)}), bf16[64,96,128]{2,1,0:T(8,128)(2,1)S(1)}, u32[]{:S(2)}, u32[]{:S(2)}) async-start(bf16[64,96,128]{2,1,0:T(8,128)(2,1)} %bitcast.28), calls=%async_computation.3 | async-start | bytes 3145728 | tf_op jit(solution)/shard_map/all_to_all | solution.py:385
  209.2 1.2 copy-start.2
  212.9 9.3 %collective-permute-start = (bf16[256,128]{1,0:T(8,128)(2,1)}, bf16[256,128]{1,0:T(8,128)(2,1)S(1)}, u32[]{:S(2)}, u32[]{:S(2)}) collective-permute-start(bf16[256,128]{1,0:T(8,128)(2,1)} %get-tuple-element.24), channel_id=1, source_target_pairs={{0,1},{1,2},{2,3},{3,0},{4,5},{5,6},{6,7},{7,4},{8,9},{9,10},{10,1... | collective-permute-start | bytes 196616 | tf_op jit(solution)/shard_map/ppermute | solution.py:400
  213.4 8.7 %collective-permute-start.1 = (bf16[256,128]{1,0:T(8,128)(2,1)}, bf16[256,128]{1,0:T(8,128)(2,1)S(1)}, u32[]{:S(2)}, u32[]{:S(2)}) collective-permute-start(bf16[256,128]{1,0:T(8,128)(2,1)} %get-tuple-element.25), channel_id=1, source_target_pairs={{0,2},{1,3},{2,0},{3,1},{4,6},{5,7},{6,4},{7,5},{8,10},{9,11},{10,... | collective-permute-start | bytes 196616 | tf_op jit(solution)/shard_map/ppermute | solution.py:400
  217.4 4.7 %collective-permute-start.2 = (bf16[256,128]{1,0:T(8,128)(2,1)}, bf16[256,128]{1,0:T(8,128)(2,1)S(1)}, u32[]{:S(2)}, u32[]{:S(2)}) collective-permute-start(bf16[256,128]{1,0:T(8,128)(2,1)} %get-tuple-element.26), channel_id=1, source_target_pairs={{0,3},{1,0},{2,1},{3,2},{4,7},{5,4},{6,5},{7,6},{8,11},{9,8},{10,9... | collective-permute-start | bytes 196616 | tf_op jit(solution)/shard_map/ppermute | solution.py:400
  217.4 12.2 %all-to-all-start.4 = ((bf16[8,56,128]{2,1,0:T(8,128)(2,1)}), bf16[8,56,128]{2,1,0:T(8,128)(2,1)S(1)}, u32[]{:S(2)}, u32[]{:S(2)}) async-start(bf16[8,56,128]{2,1,0:T(8,128)(2,1)} %bitcast.11), calls=%async_computation.4 | async-start | bytes 229376 | tf_op jit(solution)/shard_map/all_to_all | solution.py:402

commit v3 on v2

--- a/solution.py
+++ b/solution.py
@@ -11,17 +11,16 @@
 EMB = 128
 BLOCK = 32
 TABLE = ("table_0", "table_1", "table_2")
-FAR = "table_0"
-NEAR = ("table_1", "table_2", "replica")
 TABLE_REPLICA = ("table_0", "table_1", "table_2", "replica")
 BF = jnp.bfloat16
 F32 = jnp.float32
-
-
-def build_kernel(first, tile, slots_ref, iota_ref, out_ref):
+XS = 4
+
+
+def build_kernel(first, tile, slots_ref, out_ref):
     base = (first + pl.program_id(0) * tile).astype(F32)
     feats, _, batch = slots_ref.shape
-    rows = iota_ref[...]
+    rows = lax.broadcasted_iota(jnp.int32, (tile, batch), 0).astype(F32).astype(BF)
 
     def one(f, carry):
         packed = slots_ref[f]
@@ -41,13 +40,11 @@
     tile = 256
     feats, _, batch = slots.shape
     bags = feats * batch
-    iota = lax.broadcasted_iota(jnp.int32, (tile, batch), 0).astype(BF)
     return pl.pallas_call(
         functools.partial(build_kernel, first, tile),
         grid=(count // tile,),
         in_specs=[
             pl.BlockSpec((feats, 8, batch), lambda i: (0, 0, 0)),
-            pl.BlockSpec((tile, batch), lambda i: (0, 0)),
         ],
         out_specs=pl.BlockSpec((tile, bags), lambda i: (i, 0)),
         out_shape=jax.ShapeDtypeStruct((count, bags), BF),
@@ -55,11 +52,13 @@
             flops=count * bags * 8, bytes_accessed=count * bags * 2, transcendentals=0
         ),
         name="build_selection",
-    )(slots, iota)
+    )(slots)
 
 
 def cross_kernel(
     near,
+    replicas,
+    me_ref,
     rows_ref,
     sel_ref,
     scale_ref,
@@ -70,12 +69,11 @@
     down_ref,
     bias_ref,
     ow_ref,
-    grads_ref,
     gpool_ref,
-    acc,
-    base_ref,
-    lines_ref,
+    own_ref,
+    *others,
 ):
+    *send_refs, acc, base_ref, lines_ref = others
     step = pl.program_id(0)
     part = lax.dot_general(
         rows_ref[...], sel_ref[...], (((0,), (0,)), ((), ())), preferred_element_type=F32
@@ -125,8 +123,13 @@
                     part = down_part[part_rows, (c - per) * EMB : (c - per + 1) * EMB]
                 else:
                     part = jnp.zeros((near, EMB), F32)
-                lines_ref[pl.ds(z * lines + c, near, stride=far * lines), :] = part
-        grads_ref[...] = lines_ref[...].astype(BF)
+                place = (z % XS) * (far // XS) + z // XS
+                lines_ref[pl.ds(place * lines + c, near, stride=far * lines), :] = part
+        for k, ref in enumerate((own_ref, *send_refs)):
+            whose = lax.rem(me_ref[0] + k, replicas)
+            for core in range(near // replicas):
+                start = pl.multiple_of((core * replicas + whose) * far * lines, far * lines)
+                ref[core] = lines_ref[pl.ds(start, far * lines), :].astype(ref.dtype)
         grad_base = grad_crossed * (gate + 1.0) + jnp.dot(
             g_low, down_ref[...], preferred_element_type=F32
         )
@@ -135,17 +138,19 @@
             gpool_ref[f * batch : (f + 1) * batch, :] = block.astype(BF)
 
 
-def cross_layer(near, rows, sel, scale, bottom, labels, up, down, bias, ow):
+def cross_layer(near, replicas, me, rows, sel, scale, bottom, labels, up, down, bias, ow):
     tile = 512
     count, bags = sel.shape
     rank, width = up.shape
     batch = bottom.shape[0]
     lines = rank * pl.cdiv(2 * width // EMB, 8) * 8
+    part = (near // replicas, lines // near, EMB)
     whole = lambda *shape: pl.BlockSpec(shape, lambda i: (0,) * len(shape))
     return pl.pallas_call(
-        functools.partial(cross_kernel, near),
+        functools.partial(cross_kernel, near, replicas),
         grid=(count // tile,),
         in_specs=[
+            pl.BlockSpec(memory_space=pltpu.SMEM),
             pl.BlockSpec((tile, EMB), lambda i: (i, 0)),
             pl.BlockSpec((tile, bags), lambda i: (i, 0)),
             whole(*scale.shape),
@@ -157,10 +162,10 @@
             whole(1, width),
             whole(1, width),
         ],
-        out_specs=[whole(lines, EMB), whole(bags, EMB)],
+        out_specs=[whole(bags, EMB)] + [whole(*part)] * replicas,
         out_shape=[
-            jax.ShapeDtypeStruct((lines, EMB), BF),
             jax.ShapeDtypeStruct((bags, EMB), BF),
+            *(jax.ShapeDtypeStruct(part, BF if k else F32) for k in range(replicas)),
         ],
         scratch_shapes=[
             pltpu.VMEM((EMB, bags), F32),
@@ -173,7 +178,7 @@
             transcendentals=batch,
         ),
         name="cross_layer",
-    )(rows, sel, scale, scale.T, bottom, labels, up, down, bias, ow)
+    )(me, rows, sel, scale, scale.T, bottom, labels, up, down, bias, ow)
 
 
 def scatter_kernel(sel_ref, grad_ref, out_ref):
@@ -325,6 +330,14 @@
     return jnp.transpose(slots, (1, 0, 2)), scale
 
 
+def permuted(parts, axis):
+    size = lax.axis_size(axis)
+    return [
+        lax.ppermute(part, axis, [(i, (i + k) % size) for i in range(size)])
+        for k, part in enumerate(parts, 1)
+    ]
+
+
 def local(
     emb_table,
     cross_up,
@@ -345,7 +358,7 @@
     owners = lax.axis_size(TABLE)
     replicas = lax.axis_size("replica")
     hot_slots = hot_blocks.shape[1]
-    rank, width = cross_up.shape
+    _, width = cross_up.shape
 
     wanted = want_blocks.reshape(owners, 1, 1)
     asked_for = lax.all_to_all(wanted, TABLE, split_axis=0, concat_axis=0, tiled=True)
@@ -361,10 +374,14 @@
     bottom = jax.nn.relu(
         jnp.dot(dense_in, bottom_weight, precision=lax.Precision.HIGHEST) + bottom_bias
     )
-    far = lax.axis_size(FAR)
-    near = lax.axis_size(NEAR)
-    grads, grad_pooled = cross_layer(
-        near,
+    me = lax.axis_index("replica").reshape(1)
+    cores = lax.axis_size("table_2")
+    xs = lax.axis_size("table_1")
+    assert xs == XS
+    grad_pooled, own, *sends = cross_layer(
+        cores * replicas,
+        replicas,
+        me,
         fetched,
         sel,
         scale,
@@ -376,32 +393,40 @@
         out_weight[None],
     )
 
-    parts = lax.all_to_all(
-        grads.reshape(near, -1, EMB), NEAR, split_axis=0, concat_axis=0, tiled=True
-    )
+    got = permuted(sends, "replica")
 
     row_grad = scatter_rows(sel, grad_pooled, BF).reshape(shares)
-    row_grad, parts = lax.optimization_barrier((row_grad, parts))
     returned = lax.all_to_all(row_grad, TABLE, split_axis=0, concat_axis=0, tiled=True)
-    nearer = parts.astype(F32).sum(axis=0).astype(BF).reshape(far, -1, EMB)
-    nearer, returned = lax.optimization_barrier((nearer, returned))
+
+    nearer = own
+    for part in got:
+        nearer = nearer + part.astype(F32)
+    nearer = nearer.reshape(cores, xs, -1, EMB)
+    x = lax.axis_index("table_1")
+    turned = [
+        lax.dynamic_index_in_dim(nearer, lax.rem(x + k, xs), 1, keepdims=False)
+        for k in range(xs)
+    ]
+    got = permuted([part.astype(BF) for part in turned[1:]], "table_1")
+    nearest = turned[0]
+    for part in got:
+        nearest = nearest + part.astype(F32)
+    nearest = nearest.astype(BF)
+    nearest, returned = lax.optimization_barrier((nearest, returned))
+
     own, *sends = collected(
-        emb_table.shape[0],
-        replicas,
-        asked_for,
-        hot_blocks[0],
-        hot_count,
-        lax.axis_index("replica").reshape(1),
-        returned,
-    )
+        emb_table.shape[0], replicas, asked_for, hot_blocks[0], hot_count, me, returned
+    )
+    got = permuted(sends, "replica")
     table_grad = own
-    for k, part in enumerate(sends, 1):
-        ring = [(i, (i + k) % replicas) for i in range(replicas)]
-        table_grad = table_grad + lax.ppermute(part, "replica", ring).astype(F32)
-
-    mine = lax.all_to_all(nearer, FAR, split_axis=0, concat_axis=0, tiled=True)
+    for part in got:
+        table_grad = table_grad + part.astype(F32)
+
+    group = ("table_2", "table_0")
+    mine = nearest.reshape(lax.axis_size(group), -1, EMB)
+    mine = lax.all_to_all(mine, group, split_axis=0, concat_axis=0, tiled=True)
     per = 2 * width // EMB
-    mine = mine.astype(F32).sum(axis=0)[:per].reshape(rank // (near * far), 2 * width)
+    mine = mine.astype(F32).sum(axis=0)[:per].reshape(1, 2 * width)
     up_grad, down_grad = mine[:, :width], mine[:, width:]
     return (up_grad, down_grad, table_grad)
 

time: 233 us -> 222 us (0.953)
  waiting for transfers between devices: 74.1 us -> 60.8 us
  starting transfers between devices: 43.4 us -> 49.4 us
  Pallas kernels: 92.4 us -> 89.2 us
    ppermute x3 -> x9, waiting for transfers between devices: 0.01 us -> 52.1 us  [permuted(): lax.ppermute(part, axis, [(i, (i + k) % size) for i in range(size)])]
    all_to_all x1, waiting for transfers between devices: 35.9 us -> 0.01 us  [local(): lax.all_to_all(row_grad, TABLE, split_axis=0, concat_axis=0, tiled=True)]
    all_to_all x2 -> x1, waiting for transfers between devices: 30.3 us -> 0.01 us  [local(): mine = lax.all_to_all(mine, group, split_axis=0, concat_axis=0, tiled=True)]
    ppermute x3 -> x9, starting transfers between devices: 4.55 us -> 15 us  [permuted(): lax.ppermute(part, axis, [(i, (i + k) % size) for i in range(size)])]
    all_to_all x2 -> x1, starting transfers between devices: 12.1 us -> 7.37 us  [local(): mine = lax.all_to_all(mine, group, split_axis=0, concat_axis=0, tiled=True)]
    pallas_call x1, Pallas kernels: 30.3 us -> 26 us  [build_selection(): pl.pallas_call(functools.partial(build_kernel, first, tile), grid=(count...]
    reduce_sum x2 -> x1, other arithmetic: 3.24 us -> 0.04 us  [local(): mine = mine.astype(F32).sum(axis=0)[:per].reshape(1, 2 * width)]
    add x1 -> x2, other arithmetic: 1.6 us -> 4.24 us  [the longest x1 2.64 us: local(): nearer = nearer + part.astype(F32)]
  transfers between devices with their start and end apart: 8 -> 13, of which waited for: 4 -> 10; matrix products, arithmetic and copies ran while one was open for 6% -> 6% of each run, Pallas kernels for 25% -> 15%
where the time goes in v3:
time: 222 us; the launch traced here: 221 us
  Pallas kernels  89.2 us (40%)
  waiting for transfers between devices  60.8 us (27%)
  starting transfers between devices  49.4 us (22%)
  local copies, waits for them, and re-layouts  11.4 us (5%)
  other arithmetic  8.07 us (4%)
    ppermute x9, waiting for transfers between devices, permuted(): lax.ppermute(part, axis, [(i, (i + k) % size) for i in range(size)])  52.1 us
    pallas_call x1, Pallas kernels, cross_layer(): pl.pallas_call(functools.partial(cross_kernel, near, replicas), grid=(cou...  31.9 us
    pallas_call x1, Pallas kernels, build_selection(): pl.pallas_call(functools.partial(build_kernel, first, tile), grid=(count...  26 us
    pallas_call x1, Pallas kernels, scatter_rows(): pl.pallas_call(scatter_kernel, grid=(count // tile,), in_specs=[pl.BlockS...  21.2 us
    ppermute x9, starting transfers between devices, permuted(): lax.ppermute(part, axis, [(i, (i + k) % size) for i in range(size)])  15 us
    all_to_all x1, starting transfers between devices, local(): lax.all_to_all(wanted, TABLE, split_axis=0, concat_axis=0, tiled=True)  11.6 us
    all_to_all x1, starting transfers between devices, local(): lax.all_to_all(row_grad, TABLE, split_axis=0, concat_axis=0, tiled=True)  9.62 us
    all_to_all x1, waiting for transfers between devices, local(): lax.all_to_all(wanted, TABLE, split_axis=0, concat_axis=0, tiled=True)  7.93 us
  transfers between devices with their start and end apart: 13, of which 10 were waited for; matrix products, arithmetic and copies ran while one was open for 6% of the time, Pallas kernels for 15%

profile of v3, /device:TPU:32, one launch (start us, length us, event | category | flops | bytes accessed | tf_op | source)
XLA Modules:
  0.0 221.1 jit_solution(11136104951874994241)
XLA Ops:
  0.6 0.0 copy-start
  0.6 1.4 copy.33
  2.0 11.6 %all-to-all-start = ((s32[64,1,1]{2,1,0:T(1,128)}), s32[64,1,1]{2,1,0:T(1,128)S(1)}, u32[]{:S(2)}, u32[]{:S(2)}) async-start(s32[64,1,1]{2,1,0:T(1,128)} %copy.33), calls=%async_computation | async-start | bytes 65536 | tf_op jit(solution)/shard_map/all_to_all | solution.py:364
  14.3 7.9 %all-to-all-done = s32[64,1,1]{2,1,0:T(1,128)S(1)} async-done(((s32[64,1,1]{2,1,0:T(1,128)}), s32[64,1,1]{2,1,0:T(1,128)S(1)}, u32[]{:S(2)}, u32[]{:S(2)}) %all-to-all-start) | async-done | bytes 288 | tf_op jit(solution)/shard_map/all_to_all | solution.py:364
  22.2 1.8 reduce.picks_ref
  24.0 2.3 %served_rows.1 = bf16[64,96,128]{2,1,0:T(8,128)(2,1)} custom-call(s32[64]{0:T(128)} %reduce.picks_ref, s32[2]{0:T(128)} %bitcast.60, s32[1]{0:T(128)S(6)} %copy.52.count_ref, bf16[1024,128]{1,0:T(8,128)(2,1)} %table_ref.1), custom_call_target="tpu_custom_call" | custom-call | tf_op jit(solution)/shard_map/served_rows/pallas_call | solution.py:226
  26.3 0.0 copy-start.6
  26.3 5.7 %all-to-all-start.1 = ((bf16[64,96,128]{2,1,0:T(8,128)(2,1)}), bf16[64,96,128]{2,1,0:T(8,128)(2,1)S(1)}, u32[]{:S(2)}, u32[]{:S(2)}) async-start(bf16[64,96,128]{2,1,0:T(8,128)(2,1)} %served_rows.1), calls=%async_computation.1 | async-start | bytes 3145728 | tf_op jit(solution)/shard_map/all_to_all | solution.py:367
  32.1 0.6 broadcast_in_dim.11.bias_ref
  32.7 0.6 broadcast_in_dim.12.ow_ref
  33.3 0.7 copy.38.labels_ref
  34.1 0.6 copy.50
  34.7 0.6 copy.49
  35.3 5.2 %bag_slots.1 = (f32[8,26,128]{2,1,0:T(8,128)}, f32[26,128]{1,0:T(8,128)}) custom-call(s32[4,26,128]{2,1,0:T(8,128)} %bitcast.56, f32[4,26,128]{2,1,0:T(8,128)} %bitcast.57, s32[26,128]{1,0:T(8,128)} %bitcast.59), custom_call_target="tpu_custom_call" | custom-call | tf_op jit(solution)/shard_map/bag_slots/pallas_call | solution.py:322
  40.6 1.6 copy.48
  42.2 1.4 copy.37
  43.6 26.0 %build_selection.1.sel_ref = bf16[6144,3328]{1,0:T(8,128)(2,1)} custom-call(f32[26,8,128]{2,1,0:T(8,128)} %bitcast.54), custom_call_target="tpu_custom_call" | custom-call | flops 163577856 | bytes 40894464 | tf_op jit(solution)/shard_map/build_selection/pallas_call | solution.py:43
  69.6 0.9 fusion.bottom_ref
  70.5 0.8 all-to-all-done.1
  71.3 1.2 copy-done.2
  72.5 31.9 %cross_layer.1 = (bf16[3328,128]{1,0:T(8,128)(2,1)}, f32[2,1792,128]{2,1,0:T(8,128)}, bf16[2,1792,128]{2,1,0:T(8,128)(2,1)}, bf16[2,1792,128]{2,1,0:T(8,128)(2,1)}, bf16[2,1792,128]{2,1,0:T(8,128)(2,1)}) custom-call(s32[1]{0:T(128)} %bitcast.me_ref, bf16[6144,128]{1,0:T(8,128)(2,1)} %bitcast.50, bf16[6144,3328]{1,0:T(8,128)(2,1)} %build_selection.1.sel_ref, ...), custom_call_target="tpu_custom_call" | custom-call | flops 6593445888 | bytes 47972352 | tf_op jit(solution)/shard_map/cross_layer/pallas_call | solution.py:149
  104.4 21.2 %scatter_rows.1 = bf16[6144,128]{1,0:T(8,128)(2,1)} custom-call(bf16[6144,3328]{1,0:T(8,128)(2,1)} %build_selection.1.sel_ref, bf16[3328,128]{1,0:T(8,128)(2,1)} %get-tuple-element.22.grad_ref), custom_call_target="tpu_custom_call" | custom-call | flops 5234491392 | bytes 40894464 | tf_op jit(solution)/shard_map/scatter_rows/pallas_call | solution.py:193
  125.6 9.6 %all-to-all-start.2 = ((bf16[64,96,128]{2,1,0:T(8,128)(2,1)}), bf16[64,96,128]{2,1,0:T(8,128)(2,1)S(1)}, u32[]{:S(2)}, u32[]{:S(2)}) async-start(bf16[64,96,128]{2,1,0:T(8,128)(2,1)} %bitcast.49), calls=%async_computation.2 | async-start | bytes 3145728 | tf_op jit(solution)/shard_map/all_to_all | solution.py:399
  135.2 1.7 collective-permute-start
  136.9 2.9 %collective-permute-start.1 = (bf16[2,1792,128]{2,1,0:T(8,128)(2,1)}, bf16[2,1792,128]{2,1,0:T(8,128)(2,1)S(1)}, u32[]{:S(2)}, u32[]{:S(2)}) collective-permute-start(bf16[2,1792,128]{2,1,0:T(8,128)(2,1)} %get-tuple-element.20), channel_id=1, source_target_pairs={{0,2},{1,3},{2,0},{3,1},{4,6},{5,7},{6,4},{7,5},{8,10},{9,11},{10,... | collective-permute-start | bytes 2752520 | tf_op jit(solution)/shard_map/ppermute | solution.py:336
  139.8 1.3 collective-permute-start.2
  141.1 18.0 %collective-permute-done = bf16[2,1792,128]{2,1,0:T(8,128)(2,1)S(1)} collective-permute-done((bf16[2,1792,128]{2,1,0:T(8,128)(2,1)}, bf16[2,1792,128]{2,1,0:T(8,128)(2,1)S(1)}, u32[]{:S(2)}, u32[]{:S(2)}) %collective-permute-start) | collective-permute-done | bytes 917536 | tf_op jit(solution)/shard_map/ppermute | solution.py:336
  159.1 20.8 %collective-permute-done.1 = bf16[2,1792,128]{2,1,0:T(8,128)(2,1)S(1)} collective-permute-done((bf16[2,1792,128]{2,1,0:T(8,128)(2,1)}, bf16[2,1792,128]{2,1,0:T(8,128)(2,1)S(1)}, u32[]{:S(2)}, u32[]{:S(2)}) %collective-permute-start.1) | collective-permute-done | bytes 917536 | tf_op jit(solution)/shard_map/ppermute | solution.py:336
  180.0 0.9 copy-done.4
  180.9 2.6 %convert_add_fusion = f32[2,1792,128]{2,1,0:T(8,128)S(1)} fusion(bf16[2,1792,128]{2,1,0:T(8,128)(2,1)} %collective-permute-done.2, bf16[2,1792,128]{2,1,0:T(8,128)(2,1)} %copy-done.4, f32[2,1792,128]{2,1,0:T(8,128)} %get-tuple-element.18, bf16[2,1792,128]{2,1,0:T(8,128)(2,1)} %copy-done.3), kind=kLoop, calls=%fused_computation | loop fusion | flops 2752512 | bytes 6422528 | tf_op jit(solution)/shard_map/add | solution.py:403
  183.6 0.9 fusion.5
  184.5 1.5 collective-permute-start.3
  186.0 1.8 collective-permute-start.5
  187.7 1.8 collective-permute-start.4
  189.5 4.1 %collective-permute-done.3 = bf16[2,448,128]{2,1,0:T(8,128)(2,1)} collective-permute-done((bf16[2,448,128]{2,1,0:T(8,128)(2,1)}, bf16[2,448,128]{2,1,0:T(8,128)(2,1)}, u32[]{:S(2)}, u32[]{:S(2)}) %collective-permute-start.3) | collective-permute-done | bytes 229408 | tf_op jit(solution)/shard_map/ppermute | solution.py:336
  193.6 3.4 %collective-permute-done.5 = bf16[2,448,128]{2,1,0:T(8,128)(2,1)} collective-permute-done((bf16[2,448,128]{2,1,0:T(8,128)(2,1)}, bf16[2,448,128]{2,1,0:T(8,128)(2,1)}, u32[]{:S(2)}, u32[]{:S(2)}) %collective-permute-start.5) | collective-permute-done | bytes 229408 | tf_op jit(solution)/shard_map/ppermute | solution.py:336
  197.0 1.6 collective-permute-done.4
  198.6 2.0 fusion.3
  200.6 7.4 %all-to-all-start.3 = ((bf16[16,56,128]{2,1,0:T(8,128)(2,1)}), bf16[16,56,128]{2,1,0:T(8,128)(2,1)S(1)}, u32[]{:S(2)}, u32[]{:S(2)}) async-start(bf16[16,56,128]{2,1,0:T(8,128)(2,1)} %bitcast.53), calls=%async_computation.3 | async-start | bytes 458752 | tf_op jit(solution)/shard_map/all_to_all | solution.py:427
  208.0 2.6 %collected.1 = (f32[256,128]{1,0:T(8,128)}, bf16[256,128]{1,0:T(8,128)(2,1)}, bf16[256,128]{1,0:T(8,128)(2,1)}, bf16[256,128]{1,0:T(8,128)(2,1)}) custom-call(s32[64]{0:T(128)} %reduce.picks_ref, s32[2]{0:T(128)} %bitcast.61, s32[1]{0:T(128)S(6)} %copy.52.count_ref, s32[1]{0:T(128)} %bitcast.me_ref, bf16[64,96,128]{2,1,0:T(8,128)(2,1)} %copy-done.1), custom_call_target="tpu_custom_call" | custom-call | tf_op jit(solution)/shard_map/collected/pallas_call | solution.py:257
  210.5 0.9 collective-permute-start.6
  211.5 2.9 %collective-permute-start.7 = (bf16[256,128]{1,0:T(8,128)(2,1)}, bf16[256,128]{1,0:T(8,128)(2,1)S(1)}, u32[]{:S(2)}, u32[]{:S(2)}) collective-permute-start(bf16[256,128]{1,0:T(8,128)(2,1)} %get-tuple-element.27), channel_id=1, source_target_pairs={{0,2},{1,3},{2,0},{3,1},{4,6},{5,7},{6,4},{7,5},{8,10},{9,11},{10,... | collective-permute-start | bytes 196616 | tf_op jit(solution)/shard_map/ppermute | solution.py:336
  214.3 0.4 collective-permute-start.8
  214.7 2.0 collective-permute-done.6
  216.7 1.3 collective-permute-done.7
  218.0 0.8 collective-permute-done.8
  218.8 1.6 convert_add_fusion.1
  220.5 0.6 fusion.7
  (26 shorter events, 0.1 us)
Async XLA Ops:
  0.6 69.0 %copy-start = (f32[128,13]{0,1:T(8,128)S(1)}, f32[128,13]{0,1:T(8,128)}, u32[]{:S(2)}) copy-start(f32[128,13]{0,1:T(8,128)} %param.22) | copy-start | bytes 19972
  2.0 20.2 %all-to-all-start = ((s32[64,1,1]{2,1,0:T(1,128)}), s32[64,1,1]{2,1,0:T(1,128)S(1)}, u32[]{:S(2)}, u32[]{:S(2)}) async-start(s32[64,1,1]{2,1,0:T(1,128)} %copy.33), calls=%async_computation | async-start | bytes 65536 | tf_op jit(solution)/shard_map/all_to_all | solution.py:364
  26.3 5.8 %copy-start.7 = (f32[3456]{0:T(1024)S(1)}, f32[3456]{0:T(1024)}, u32[]{:S(2)}) copy-start(f32[3456]{0:T(1024)} %param.18) | copy-start | bytes 41476
  26.3 6.4 %copy-start.8 = (f32[3456]{0:T(1024)S(1)}, f32[3456]{0:T(1024)}, u32[]{:S(2)}) copy-start(f32[3456]{0:T(1024)} %param.19) | copy-start | bytes 41476
  26.3 7.0 %copy-start.10 = (s32[128]{0:T(128)S(1)}, s32[128]{0:T(128)}, u32[]{:S(2)}) copy-start(s32[128]{0:T(128)} %param.23) | copy-start | bytes 1540
  26.3 7.7 %copy-start.5 = (s32[128,26,4]{0,2,1:T(4,128)S(1)}, s32[128,26,4]{0,2,1:T(4,128)}, u32[]{:S(2)}) copy-start(s32[128,26,4]{0,2,1:T(4,128)} %param.24) | copy-start | bytes 159748
  26.3 8.4 %copy-start.6 = (f32[128,26,4]{0,2,1:T(4,128)S(1)}, f32[128,26,4]{0,2,1:T(4,128)}, u32[]{:S(2)}) copy-start(f32[128,26,4]{0,2,1:T(4,128)} %param.25) | copy-start | bytes 159748
  26.3 44.9 %all-to-all-start.1 = ((bf16[64,96,128]{2,1,0:T(8,128)(2,1)}), bf16[64,96,128]{2,1,0:T(8,128)(2,1)S(1)}, u32[]{:S(2)}, u32[]{:S(2)}) async-start(bf16[64,96,128]{2,1,0:T(8,128)(2,1)} %served_rows.1), calls=%async_computation.1 | async-start | bytes 3145728 | tf_op jit(solution)/shard_map/all_to_all | solution.py:367
  43.6 26.0 %copy-start.9 = (f32[13,128]{1,0:T(8,128)S(1)}, f32[13,128]{1,0:T(8,128)}, u32[]{:S(2)}) copy-start(f32[13,128]{1,0:T(8,128)} %param.20) | copy-start | bytes 19972
  43.6 26.0 %copy-start.11 = (f32[128]{0:T(128)S(1)}, f32[128]{0:T(128)}, u32[]{:S(2)}) copy-start(f32[128]{0:T(128)} %param.21) | copy-start | bytes 1540
  71.3 1.2 copy-start.2
  125.6 75.0 %all-to-all-start.2 = ((bf16[64,96,128]{2,1,0:T(8,128)(2,1)}), bf16[64,96,128]{2,1,0:T(8,128)(2,1)S(1)}, u32[]{:S(2)}, u32[]{:S(2)}) async-start(bf16[64,96,128]{2,1,0:T(8,128)(2,1)} %bitcast.49), calls=%async_computation.2 | async-start | bytes 3145728 | tf_op jit(solution)/shard_map/all_to_all | solution.py:399
  135.2 23.9 %collective-permute-start = (bf16[2,1792,128]{2,1,0:T(8,128)(2,1)}, bf16[2,1792,128]{2,1,0:T(8,128)(2,1)S(1)}, u32[]{:S(2)}, u32[]{:S(2)}) collective-permute-start(bf16[2,1792,128]{2,1,0:T(8,128)(2,1)} %get-tuple-element.19), channel_id=1, source_target_pairs={{0,1},{1,2},{2,3},{3,0},{4,5},{5,6},{6,7},{7,4},{8,9},{9,10},{10,1... | collective-permute-start | bytes 2752520 | tf_op jit(solution)/shard_map/ppermute | solution.py:336
  136.9 43.1 %collective-permute-start.1 = (bf16[2,1792,128]{2,1,0:T(8,128)(2,1)}, bf16[2,1792,128]{2,1,0:T(8,128)(2,1)S(1)}, u32[]{:S(2)}, u32[]{:S(2)}) collective-permute-start(bf16[2,1792,128]{2,1,0:T(8,128)(2,1)} %get-tuple-element.20), channel_id=1, source_target_pairs={{0,2},{1,3},{2,0},{3,1},{4,6},{5,7},{6,4},{7,5},{8,10},{9,11},{10,... | collective-permute-start | bytes 2752520 | tf_op jit(solution)/shard_map/ppermute | solution.py:336
  139.8 40.2 %collective-permute-start.2 = (bf16[2,1792,128]{2,1,0:T(8,128)(2,1)}, bf16[2,1792,128]{2,1,0:T(8,128)(2,1)}, u32[]{:S(2)}, u32[]{:S(2)}) collective-permute-start(bf16[2,1792,128]{2,1,0:T(8,128)(2,1)} %get-tuple-element.21), channel_id=1, source_target_pairs={{0,3},{1,0},{2,1},{3,2},{4,7},{5,4},{6,5},{7,6},{8,11},{9,8},{10,9... | collective-permute-start | bytes 2752520 | tf_op jit(solution)/shard_map/ppermute | solution.py:336
  159.1 20.8 %copy-start.3 = (bf16[2,1792,128]{2,1,0:T(8,128)(2,1)}, bf16[2,1792,128]{2,1,0:T(8,128)(2,1)S(1)}, u32[]{:S(2)}) copy-start(bf16[2,1792,128]{2,1,0:T(8,128)(2,1)S(1)} %collective-permute-done) | copy-start | bytes 2752516
  180.0 0.9 copy-start.4
  184.5 9.1 %collective-permute-start.3 = (bf16[2,448,128]{2,1,0:T(8,128)(2,1)}, bf16[2,448,128]{2,1,0:T(8,128)(2,1)}, u32[]{:S(2)}, u32[]{:S(2)}) collective-permute-start(bf16[2,448,128]{2,1,0:T(8,128)(2,1)} %get-tuple-element.29), channel_id=1, source_target_pairs={{0,8},{8,16},{16,24},{24,0},{1,9},{9,17},{17,25},{25,1},{2,10},{10... | collective-permute-start | bytes 688136 | tf_op jit(solution)/shard_map/ppermute | solution.py:336
  186.0 11.0 %collective-permute-start.5 = (bf16[2,448,128]{2,1,0:T(8,128)(2,1)}, bf16[2,448,128]{2,1,0:T(8,128)(2,1)}, u32[]{:S(2)}, u32[]{:S(2)}) collective-permute-start(bf16[2,448,128]{2,1,0:T(8,128)(2,1)} %get-tuple-element.30), channel_id=1, source_target_pairs={{0,24},{8,0},{16,8},{24,16},{1,25},{9,1},{17,9},{25,17},{2,26},{10... | collective-permute-start | bytes 688136 | tf_op jit(solution)/shard_map/ppermute | solution.py:336
  187.7 10.9 %collective-permute-start.4 = (bf16[2,448,128]{2,1,0:T(8,128)(2,1)}, bf16[2,448,128]{2,1,0:T(8,128)(2,1)}, u32[]{:S(2)}, u32[]{:S(2)}) collective-permute-start(bf16[2,448,128]{2,1,0:T(8,128)(2,1)} %get-tuple-element.31), channel_id=1, source_target_pairs={{0,16},{8,24},{16,0},{24,8},{1,17},{9,25},{17,1},{25,9},{2,18},{10... | collective-permute-start | bytes 688136 | tf_op jit(solution)/shard_map/ppermute | solution.py:336
  200.6 7.4 %copy-start.1 = (bf16[64,96,128]{2,1,0:T(8,128)(2,1)}, bf16[64,96,128]{2,1,0:T(8,128)(2,1)S(1)}, u32[]{:S(2)}) copy-start(bf16[64,96,128]{2,1,0:T(8,128)(2,1)S(1)} %all-to-all-done.2.back_ref) | copy-start | bytes 4718596
  200.6 19.8 %all-to-all-start.3 = ((bf16[16,56,128]{2,1,0:T(8,128)(2,1)}), bf16[16,56,128]{2,1,0:T(8,128)(2,1)S(1)}, u32[]{:S(2)}, u32[]{:S(2)}) async-start(bf16[16,56,128]{2,1,0:T(8,128)(2,1)} %bitcast.53), calls=%async_computation.3 | async-start | bytes 458752 | tf_op jit(solution)/shard_map/all_to_all | solution.py:427
  210.5 6.1 %collective-permute-start.6 = (bf16[256,128]{1,0:T(8,128)(2,1)}, bf16[256,128]{1,0:T(8,128)(2,1)S(1)}, u32[]{:S(2)}, u32[]{:S(2)}) collective-permute-start(bf16[256,128]{1,0:T(8,128)(2,1)} %get-tuple-element.26), channel_id=1, source_target_pairs={{0,1},{1,2},{2,3},{3,0},{4,5},{5,6},{6,7},{7,4},{8,9},{9,10},{10,1... | collective-permute-start | bytes 196616 | tf_op jit(solution)/shard_map/ppermute | solution.py:336
  211.5 6.6 %collective-permute-start.7 = (bf16[256,128]{1,0:T(8,128)(2,1)}, bf16[256,128]{1,0:T(8,128)(2,1)S(1)}, u32[]{:S(2)}, u32[]{:S(2)}) collective-permute-start(bf16[256,128]{1,0:T(8,128)(2,1)} %get-tuple-element.27), channel_id=1, source_target_pairs={{0,2},{1,3},{2,0},{3,1},{4,6},{5,7},{6,4},{7,5},{8,10},{9,11},{10,... | collective-permute-start | bytes 196616 | tf_op jit(solution)/shard_map/ppermute | solution.py:336
  214.3 4.5 %collective-permute-start.8 = (bf16[256,128]{1,0:T(8,128)(2,1)}, bf16[256,128]{1,0:T(8,128)(2,1)S(1)}, u32[]{:S(2)}, u32[]{:S(2)}) collective-permute-start(bf16[256,128]{1,0:T(8,128)(2,1)} %get-tuple-element.28), channel_id=1, source_target_pairs={{0,3},{1,0},{2,1},{3,2},{4,7},{5,4},{6,5},{7,6},{8,11},{9,8},{10,9... | collective-permute-start | bytes 196616 | tf_op jit(solution)/shard_map/ppermute | solution.py:336

commit v4 on v3

--- a/solution.py
+++ b/solution.py
@@ -55,12 +55,63 @@
     )(slots)
 
 
+def build_hot_kernel(first, tile, me_ref, slots_ref, rows_ref, sel_ref, pooled_ref):
+    build_kernel(first, tile, slots_ref, sel_ref)
+    part = lax.dot_general(
+        rows_ref[...], sel_ref[...], (((0,), (0,)), ((), ())), preferred_element_type=F32
+    )
+
+    @pl.when(pl.program_id(0) == 0)
+    def _():
+        pooled_ref[...] = part
+
+    @pl.when(pl.program_id(0) > 0)
+    def _():
+        pooled_ref[...] += part
+
+
+def build_hot(me, slots, pieces, first, replicas):
+    tile = 256
+    feats, _, batch = slots.shape
+    bags = feats * batch
+    count = pieces.shape[0]
+    per = count // replicas // tile
+
+    def rows_map(i, me):
+        return lax.rem(me[0] - i // per + replicas, replicas) * per + i % per, 0
+
+    return pl.pallas_call(
+        functools.partial(build_hot_kernel, first, tile),
+        grid_spec=pltpu.PrefetchScalarGridSpec(
+            num_scalar_prefetch=1,
+            grid=(count // tile,),
+            in_specs=[
+                pl.BlockSpec((feats, 8, batch), lambda i, me: (0, 0, 0)),
+                pl.BlockSpec((tile, EMB), rows_map),
+            ],
+            out_specs=[
+                pl.BlockSpec((tile, bags), lambda i, me: (i, 0)),
+                pl.BlockSpec((EMB, bags), lambda i, me: (0, 0)),
+            ],
+        ),
+        out_shape=[
+            jax.ShapeDtypeStruct((count, bags), BF),
+            jax.ShapeDtypeStruct((EMB, bags), F32),
+        ],
+        cost_estimate=pl.CostEstimate(
+            flops=count * bags * 256, bytes_accessed=count * bags * 2, transcendentals=0
+        ),
+        name="build_hot",
+    )(me, slots, pieces)
+
+
 def cross_kernel(
     near,
     replicas,
     me_ref,
     rows_ref,
     sel_ref,
+    hot_ref,
     scale_ref,
     scale_t_ref,
     bottom_ref,
@@ -81,7 +132,7 @@
 
     @pl.when(step == 0)
     def _():
-        acc[...] = part
+        acc[...] = hot_ref[...] + part
 
     @pl.when(step > 0)
     def _():
@@ -138,7 +189,7 @@
             gpool_ref[f * batch : (f + 1) * batch, :] = block.astype(BF)
 
 
-def cross_layer(near, replicas, me, rows, sel, scale, bottom, labels, up, down, bias, ow):
+def cross_layer(near, replicas, me, rows, sel, hot, scale, bottom, labels, up, down, bias, ow):
     tile = 512
     count, bags = sel.shape
     rank, width = up.shape
@@ -153,6 +204,7 @@
             pl.BlockSpec(memory_space=pltpu.SMEM),
             pl.BlockSpec((tile, EMB), lambda i: (i, 0)),
             pl.BlockSpec((tile, bags), lambda i: (i, 0)),
+            whole(EMB, bags),
             whole(*scale.shape),
             whole(batch, scale.shape[0]),
             whole(batch, EMB),
@@ -178,57 +230,82 @@
             transcendentals=batch,
         ),
         name="cross_layer",
-    )(me, rows, sel, scale, scale.T, bottom, labels, up, down, bias, ow)
-
-
-def scatter_kernel(sel_ref, grad_ref, out_ref):
-    out_ref[...] = jnp.dot(
-        sel_ref[...], grad_ref[...], preferred_element_type=F32
-    ).astype(out_ref.dtype)
-
-
-def scatter_rows(sel, grad, dtype):
-    tile = 512
-    count, bags = sel.shape
+    )(me, rows, sel, hot, scale, scale.T, bottom, labels, up, down, bias, ow)
+
+
+def scatter_kernel(cold_ref, hot_ref, grad_ref, out_ref):
+    grad = grad_ref[...]
+    some = out_ref.shape[0]
+    cold = jnp.dot(cold_ref[...], grad, preferred_element_type=F32).astype(BF)
+    out_ref[:, :BLOCK, :] = cold.reshape(some, BLOCK, EMB)
+    for piece in range(hot_ref.shape[0]):
+        part = jnp.dot(hot_ref[piece], grad, preferred_element_type=F32).astype(BF)
+        share = part.shape[0] // some
+        start = BLOCK + piece * share
+        out_ref[:, start : start + share, :] = part.reshape(some, share, EMB)
+
+
+def scatter_rows(cold, hot, grad, owners, pieces):
+    some = 8
+    bags = cold.shape[1]
+    share = hot.shape[0] // (owners * pieces)
+    each = BLOCK + pieces * share
     return pl.pallas_call(
         scatter_kernel,
-        grid=(count // tile,),
+        grid=(owners // some,),
         in_specs=[
-            pl.BlockSpec((tile, bags), lambda i: (i, 0)),
+            pl.BlockSpec((some * BLOCK, bags), lambda i: (i, 0)),
+            pl.BlockSpec((pieces, some * share, bags), lambda i: (0, i, 0)),
             pl.BlockSpec((bags, EMB), lambda i: (0, 0)),
         ],
-        out_specs=pl.BlockSpec((tile, EMB), lambda i: (i, 0)),
-        out_shape=jax.ShapeDtypeStruct((count, EMB), dtype),
+        out_specs=pl.BlockSpec((some, each, EMB), lambda i: (i, 0, 0)),
+        out_shape=jax.ShapeDtypeStruct((owners, each, EMB), BF),
         cost_estimate=pl.CostEstimate(
-            flops=2 * count * bags * EMB, bytes_accessed=count * bags * 2, transcendentals=0
+            flops=2 * owners * each * bags * EMB,
+            bytes_accessed=owners * each * bags * 2,
+            transcendentals=0,
         ),
         name="scatter_rows",
-    )(sel, grad)
-
-
-def serve_kernel(picks_ref, hot_picks_ref, count_ref, table_ref, out_ref):
-    hot = []
-    for s in range(hot_picks_ref.shape[0]):
-        start = pl.multiple_of(hot_picks_ref[s] * BLOCK, BLOCK)
-        rows = table_ref[pl.ds(start, BLOCK), :]
-        hot.append(jnp.where(s < count_ref[0], rows, jnp.zeros_like(rows)))
+    )(cold, hot.reshape(pieces, owners * share, bags), grad)
+
+
+def hot_kernel(picks_ref, count_ref, me_ref, table_ref, out_ref):
+    peers, share, _ = out_ref.shape
+    shares = BLOCK // share
+    slot, part = lax.div(me_ref[0], shares), lax.rem(me_ref[0], shares)
+    start = pl.multiple_of(picks_ref[slot] * BLOCK + part * share, share)
+    rows = table_ref[pl.ds(start, share), :]
+    rows = jnp.where(slot < count_ref[0], rows, jnp.zeros_like(rows))
+    for i in range(peers):
+        out_ref[i] = rows
+
+
+def hot_share(emb_table, peers, share, picks, count, me):
+    smem = pl.BlockSpec(memory_space=pltpu.SMEM)
+    vmem = pl.BlockSpec(memory_space=pltpu.VMEM)
+    return pl.pallas_call(
+        hot_kernel,
+        in_specs=[smem, smem, smem, vmem],
+        out_shape=jax.ShapeDtypeStruct((peers, share, EMB), BF),
+        name="hot_share",
+    )(picks, count, me, emb_table)
+
+
+def serve_kernel(picks_ref, table_ref, out_ref):
     for i in range(out_ref.shape[0]):
         start = pl.multiple_of(picks_ref[i] * BLOCK, BLOCK)
-        out_ref[i, :BLOCK, :] = table_ref[pl.ds(start, BLOCK), :]
-        for s, rows in enumerate(hot):
-            out_ref[i, (s + 1) * BLOCK : (s + 2) * BLOCK, :] = rows
-
-
-def served_rows(emb_table, picks, hot_picks, count):
+        out_ref[i] = table_ref[pl.ds(start, BLOCK), :]
+
+
+def served_rows(emb_table, picks):
     smem = pl.BlockSpec(memory_space=pltpu.SMEM)
     vmem = pl.BlockSpec(memory_space=pltpu.VMEM)
-    share = (1 + hot_picks.shape[0]) * BLOCK
     return pl.pallas_call(
         serve_kernel,
-        in_specs=[smem, smem, smem, vmem],
-        out_shape=jax.ShapeDtypeStruct((picks.shape[0], share, EMB), BF),
+        in_specs=[smem, vmem],
+        out_shape=jax.ShapeDtypeStruct((picks.shape[0], BLOCK, EMB), BF),
         name="served_rows",
-    )(picks, hot_picks, count, emb_table)
+    )(picks, emb_table)
 
 
 def collect_kernel(picks_ref, hot_picks_ref, count_ref, me_ref, back_ref, own_ref, *others):
@@ -265,17 +342,21 @@
     )(picks, hot_picks, count, me, back)
 
 
-def slots_kernel(cold, hot_slots, tries, ids_ref, weight_ref, length_ref, slots_ref, scale_ref):
+def slots_kernel(cold, share, tries, ids_ref, weight_ref, length_ref, slots_ref, scale_ref):
     bag = ids_ref.shape[0]
     length = length_ref[...]
     row_bits = BLOCK.bit_length() - 1
     cold_bits = cold.bit_length() - 1
+    share_bits = share.bit_length() - 1
     ids, coef = [], []
     for s in range(bag):
         i = ids_ref[s]
-        slot, rest = i >> cold_bits, i & (cold - 1)
-        owner, row = rest >> row_bits, rest & (BLOCK - 1)
-        ids.append((owner * (1 + hot_slots) + slot) * BLOCK + row)
+        h = i - cold
+        slot, rest = h >> cold_bits, h & (cold - 1)
+        owner, row = rest >> row_bits, (slot << row_bits) + (rest & (BLOCK - 1))
+        piece, row = row >> share_bits, row & (share - 1)
+        moved = cold + piece * (cold // BLOCK * share) + owner * share + row
+        ids.append(jnp.where(i < cold, i, moved))
         coef.append(jnp.where(s < length, weight_ref[s], 0.0))
     total = []
     for j in range(bag):
@@ -316,11 +397,11 @@
     scale_ref[...] = scale
 
 
-def bag_slots(ids, weight, length, owners, hot_slots):
+def bag_slots(ids, weight, length, owners, share):
     cold = owners * BLOCK
     batch, feats, bag = ids.shape
     slots, scale = pl.pallas_call(
-        functools.partial(slots_kernel, cold, hot_slots, 64),
+        functools.partial(slots_kernel, cold, share, 64),
         out_shape=[
             jax.ShapeDtypeStruct((2 * bag, feats, batch), F32),
             jax.ShapeDtypeStruct((feats, batch), F32),
@@ -360,21 +441,27 @@
     hot_slots = hot_blocks.shape[1]
     _, width = cross_up.shape
 
-    wanted = want_blocks.reshape(owners, 1, 1)
+    me = lax.axis_index("replica").reshape(1)
+    share = hot_slots * BLOCK // replicas
+    own_hot = hot_share(emb_table, owners, share, hot_blocks[0], hot_count, me)
+    piece = lax.all_to_all(own_hot, TABLE, split_axis=0, concat_axis=0, tiled=True)
+    piece = piece.reshape(-1, EMB)
+    pieces = jnp.concatenate([piece, *permuted([piece] * (replicas - 1), "replica")], 0)
+
+    wanted, piece = lax.optimization_barrier((want_blocks.reshape(owners, 1, 1), piece))
     asked_for = lax.all_to_all(wanted, TABLE, split_axis=0, concat_axis=0, tiled=True)
     asked_for = asked_for.reshape(owners)
-    served = served_rows(emb_table, asked_for, hot_blocks[0], hot_count)
+    served = served_rows(emb_table, asked_for)
     fetched = lax.all_to_all(served, TABLE, split_axis=0, concat_axis=0, tiled=True)
-    shares = fetched.shape
     fetched = fetched.reshape(-1, EMB)
 
-    slots, scale = bag_slots(lookup_ids, bag_weight, bag_length, owners, hot_slots)
+    slots, scale = bag_slots(lookup_ids, bag_weight, bag_length, owners, share)
     sel = build_selection(slots, 0, fetched.shape[0])
+    sel_hot, pooled_hot = build_hot(me, slots, pieces, fetched.shape[0], replicas)
 
     bottom = jax.nn.relu(
         jnp.dot(dense_in, bottom_weight, precision=lax.Precision.HIGHEST) + bottom_bias
     )
-    me = lax.axis_index("replica").reshape(1)
     cores = lax.axis_size("table_2")
     xs = lax.axis_size("table_1")
     assert xs == XS
@@ -384,6 +471,7 @@
         me,
         fetched,
         sel,
+        pooled_hot,
         scale,
         bottom,
         labels[:, None],
@@ -395,7 +483,7 @@
 
     got = permuted(sends, "replica")
 
-    row_grad = scatter_rows(sel, grad_pooled, BF).reshape(shares)
+    row_grad = scatter_rows(sel, sel_hot, grad_pooled, owners, replicas)
     returned = lax.all_to_all(row_grad, TABLE, split_axis=0, concat_axis=0, tiled=True)
 
     nearer = own

time: 222 us -> 242 us (1.090)
  blocking collectives: 0 us -> 23.8 us
  Pallas kernels: 89.2 us -> 86.1 us
    pallas_call x3 -> x5, Pallas kernels: 28.7 us -> 53.5 us  [the longest x1 25.5 us: build_hot(): pl.pallas_call(functools.partial(build_hot_kernel, first, tile), grid_spe...]
    all_to_all x0 -> x1, blocking collectives: none -> 23.8 us  [local(): lax.all_to_all(own_hot, TABLE, split_axis=0, concat_axis=0, tiled=True)]
    pallas_call x1, Pallas kernels: 26 us -> 9.77 us  [build_selection(): pl.pallas_call(functools.partial(build_kernel, first, tile), grid=(count...]
    pallas_call x1, Pallas kernels: 31.9 us -> 20.3 us  [cross_layer(): pl.pallas_call(functools.partial(cross_kernel, near, replicas), grid=(cou...]
    all_to_all x1, starting transfers between devices: 11.6 us -> 5.64 us  [local(): lax.all_to_all(wanted, TABLE, split_axis=0, concat_axis=0, tiled=True)]
    all_to_all x1, waiting for transfers between devices: 7.93 us -> 3.59 us  [local(): lax.all_to_all(wanted, TABLE, split_axis=0, concat_axis=0, tiled=True)]
    ppermute x9 -> x12, starting transfers between devices: 15 us -> 18.3 us  [permuted(): lax.ppermute(part, axis, [(i, (i + k) % size) for i in range(size)])]
    ppermute x9 -> x12, waiting for transfers between devices: 52.1 us -> 54.9 us  [permuted(): lax.ppermute(part, axis, [(i, (i + k) % size) for i in range(size)])]
  transfers between devices with their start and end apart: 13 -> 16, of which waited for: 10 -> 8; matrix products, arithmetic and copies ran while one was open for 6% -> 8% of each run, Pallas kernels for 15% -> 19%
where the time goes in v4:
time: 242 us; the launch traced here: 241 us
  Pallas kernels  86.1 us (36%)
  waiting for transfers between devices  58.4 us (24%)
  starting transfers between devices  48.4 us (20%)
  blocking collectives  23.8 us (10%)
  local copies, waits for them, and re-layouts  12.2 us (5%)
  other arithmetic  9.23 us (4%)
    ppermute x12, waiting for transfers between devices, permuted(): lax.ppermute(part, axis, [(i, (i + k) % size) for i in range(size)])  54.9 us
    pallas_call x1, Pallas kernels, build_hot(): pl.pallas_call(functools.partial(build_hot_kernel, first, tile), grid_spe...  25.5 us
    all_to_all x1, blocking collectives, local(): lax.all_to_all(own_hot, TABLE, split_axis=0, concat_axis=0, tiled=True)  23.8 us
    pallas_call x1, Pallas kernels, cross_layer(): pl.pallas_call(functools.partial(cross_kernel, near, replicas), grid=(cou...  20.3 us
    pallas_call x1, Pallas kernels, scatter_rows(): pl.pallas_call(scatter_kernel, grid=(owners // some,), in_specs=[pl.Block...  19.2 us
    ppermute x12, starting transfers between devices, permuted(): lax.ppermute(part, axis, [(i, (i + k) % size) for i in range(size)])  18.3 us
    all_to_all x1, starting transfers between devices, local(): lax.all_to_all(row_grad, TABLE, split_axis=0, concat_axis=0, tiled=True)  10.3 us
    pallas_call x1, Pallas kernels, build_selection(): pl.pallas_call(functools.partial(build_kernel, first, tile), grid=(count...  9.77 us
  transfers between devices with their start and end apart: 16, of which 8 were waited for; matrix products, arithmetic and copies ran while one was open for 8% of the time, Pallas kernels for 19%

profile of v4, /device:TPU:32, one launch (start us, length us, event | category | flops | bytes accessed | tf_op | source)
XLA Modules:
  0.0 240.6 jit_solution(1328884464900557859)
XLA Ops:
  1.4 1.7 hot_share.1
  3.1 23.8 %all_to_all.25 = bf16[64,16,128]{2,1,0:T(8,128)(2,1)S(1)} all-to-all(bf16[64,16,128]{2,1,0:T(8,128)(2,1)} %hot_share.1), channel_id=1, replica_groups=mesh['table_0'=8,'table_1'=4,'table_2'=2,'replica'=4] {'table_0','table_..., dimensions={0} | all-to-all | bytes 524288 | tf_op jit(solution)/shard_map/all_to_all | solution.py:447
  26.9 1.6 collective-permute-start
  28.4 2.9 %collective-permute-start.1 = (bf16[1024,128]{1,0:T(8,128)(2,1)S(1)}, bf16[1024,128]{1,0:T(8,128)(2,1)S(1)}, u32[]{:S(2)}, u32[]{:S(2)}) collective-permute-start(bf16[1024,128]{1,0:T(8,128)(2,1)S(1)} %bitcast.55), channel_id=1, source_target_pairs={{0,2},{1,3},{2,0},{3,1},{4,6},{5,7},{6,4},{7,5},{8,10},{9,11},{10,... | collective-permute-start | bytes 786440 | tf_op jit(solution)/shard_map/ppermute | solution.py:417
  31.3 1.3 collective-permute-start.2
  32.7 1.4 copy.49
  34.1 1.4 copy.50
  35.6 5.2 %bag_slots.1 = (f32[8,26,128]{2,1,0:T(8,128)}, f32[26,128]{1,0:T(8,128)}) custom-call(s32[4,26,128]{2,1,0:T(8,128)} %bitcast.63, f32[4,26,128]{2,1,0:T(8,128)} %bitcast.62, s32[26,128]{1,0:T(8,128)} %bitcast.65), custom_call_target="tpu_custom_call" | custom-call | tf_op jit(solution)/shard_map/bag_slots/pallas_call | solution.py:403
  40.8 1.3 copy.33
  42.2 5.6 %all-to-all-start.1 = ((s32[64,1,1]{2,1,0:T(1,128)}), s32[64,1,1]{2,1,0:T(1,128)S(1)}, u32[]{:S(2)}, u32[]{:S(2)}) async-start(s32[64,1,1]{2,1,0:T(1,128)} %copy.33), calls=%async_computation.1 | async-start | bytes 65536 | tf_op jit(solution)/shard_map/all_to_all | solution.py:452
  47.8 1.6 copy.48
  49.4 1.4 copy.37
  50.9 0.7 copy.38.labels_ref
  51.6 0.6 broadcast_in_dim.11.bias_ref
  52.2 0.6 broadcast_in_dim.12.ow_ref
  52.8 3.6 %all-to-all-done.1 = s32[64,1,1]{2,1,0:T(1,128)S(1)} async-done(((s32[64,1,1]{2,1,0:T(1,128)}), s32[64,1,1]{2,1,0:T(1,128)S(1)}, u32[]{:S(2)}, u32[]{:S(2)}) %all-to-all-start.1) | async-done | bytes 288 | tf_op jit(solution)/shard_map/all_to_all | solution.py:452
  56.4 1.8 reduce.picks_ref
  58.3 1.9 served_rows.1
  60.1 6.7 %all-to-all-start.2 = ((bf16[64,32,128]{2,1,0:T(8,128)(2,1)}), bf16[64,32,128]{2,1,0:T(8,128)(2,1)S(1)}, u32[]{:S(2)}, u32[]{:S(2)}) async-start(bf16[64,32,128]{2,1,0:T(8,128)(2,1)} %served_rows.1), calls=%async_computation.2 | async-start | bytes 1048576 | tf_op jit(solution)/shard_map/all_to_all | solution.py:455
  66.9 9.8 %build_selection.1.sel_ref.cold_ref = bf16[2048,3328]{1,0:T(8,128)(2,1)} custom-call(f32[26,8,128]{2,1,0:T(8,128)} %bitcast.59), custom_call_target="tpu_custom_call" | custom-call | flops 54525952 | bytes 13631488 | tf_op jit(solution)/shard_map/build_selection/pallas_call | solution.py:43
  76.6 0.9 fusion.bottom_ref
  77.6 1.1 pad_maximum_fusion.rows_ref
  78.7 25.5 %build_hot.1 = (bf16[4096,3328]{1,0:T(8,128)(2,1)}, f32[128,3328]{1,0:T(8,128)}) custom-call(s32[1]{0:T(128)} %bitcast.me_ref, f32[26,8,128]{2,1,0:T(8,128)} %bitcast.60, bf16[4096,128]{1,0:T(8,128)(2,1)} %pad_maximum_fusion.rows_ref), custom_call_target="tpu_custom_call" | custom-call | flops 3489660928 | bytes 27262976 | tf_op jit(solution)/shard_map/build_hot/pallas_call | solution.py:83
  104.3 0.8 copy-done.2
  105.1 20.3 %cross_layer.1 = (bf16[3328,128]{1,0:T(8,128)(2,1)}, f32[2,1792,128]{2,1,0:T(8,128)}, bf16[2,1792,128]{2,1,0:T(8,128)(2,1)}, bf16[2,1792,128]{2,1,0:T(8,128)(2,1)}, bf16[2,1792,128]{2,1,0:T(8,128)(2,1)}) custom-call(s32[1]{0:T(128)} %bitcast.me_ref, bf16[2048,128]{1,0:T(8,128)(2,1)} %bitcast.53, bf16[2048,3328]{1,0:T(8,128)(2,1)} %build_selection.1.sel_ref.cold_ref, ...), custom_call_target="tpu_custom_call" | custom-call | flops 3103784960 | bytes 20709376 | tf_op jit(solution)/shard_map/cross_layer/pallas_call | solution.py:200
  125.4 19.2 %scatter_rows.1 = bf16[64,96,128]{2,1,0:T(8,128)(2,1)} custom-call(bf16[2048,3328]{1,0:T(8,128)(2,1)} %build_selection.1.sel_ref.cold_ref, bf16[4,1024,3328]{2,1,0:T(8,128)(2,1)} %bitcast.50, bf16[3328,128]{1,0:T(8,128)(2,1)} %get-tuple-element.28.grad_ref), custom_call_target="tpu_custom_call" | custom-call | flops 5234491392 | bytes 40894464 | tf_op jit(solution)/shard_map/scatter_rows/pallas_call | solution.py:253
  144.5 10.3 %all-to-all-start.3 = ((bf16[64,96,128]{2,1,0:T(8,128)(2,1)}), bf16[64,96,128]{2,1,0:T(8,128)(2,1)S(1)}, u32[]{:S(2)}, u32[]{:S(2)}) async-start(bf16[64,96,128]{2,1,0:T(8,128)(2,1)} %scatter_rows.1), calls=%async_computation.3 | async-start | bytes 3145728 | tf_op jit(solution)/shard_map/all_to_all | solution.py:487
  154.9 0.7 collective-permute-start.3
  155.6 0.8 collective-permute-start.4
  156.4 2.0 collective-permute-start.5
  158.4 40.1 %collective-permute-done.3 = bf16[2,1792,128]{2,1,0:T(8,128)(2,1)S(1)} collective-permute-done((bf16[2,1792,128]{2,1,0:T(8,128)(2,1)}, bf16[2,1792,128]{2,1,0:T(8,128)(2,1)S(1)}, u32[]{:S(2)}, u32[]{:S(2)}) %collective-permute-start.3) | collective-permute-done | bytes 917536 | tf_op jit(solution)/shard_map/ppermute | solution.py:417
  198.4 0.7 collective-permute-done.5
  199.7 2.6 %convert_add_fusion = f32[2,1792,128]{2,1,0:T(8,128)S(1)} fusion(bf16[2,1792,128]{2,1,0:T(8,128)(2,1)} %collective-permute-done.5, bf16[2,1792,128]{2,1,0:T(8,128)(2,1)} %copy-done.4, f32[2,1792,128]{2,1,0:T(8,128)} %get-tuple-element.23, bf16[2,1792,128]{2,1,0:T(8,128)(2,1)} %copy-done.3), kind=kLoop, calls=%fused_computation | loop fusion | flops 2752512 | bytes 6422528 | tf_op jit(solution)/shard_map/add | solution.py:491
  202.3 0.9 fusion.5
  203.2 1.5 collective-permute-start.6
  204.7 2.7 %collective-permute-start.7 = (bf16[2,448,128]{2,1,0:T(8,128)(2,1)}, bf16[2,448,128]{2,1,0:T(8,128)(2,1)}, u32[]{:S(2)}, u32[]{:S(2)}) collective-permute-start(bf16[2,448,128]{2,1,0:T(8,128)(2,1)} %get-tuple-element.37), channel_id=1, source_target_pairs={{0,16},{8,24},{16,0},{24,8},{1,17},{9,25},{17,1},{25,9},{2,18},{10... | collective-permute-start | bytes 688136 | tf_op jit(solution)/shard_map/ppermute | solution.py:417
  207.4 1.5 collective-permute-start.8
  208.8 3.5 %collective-permute-done.6 = bf16[2,448,128]{2,1,0:T(8,128)(2,1)} collective-permute-done((bf16[2,448,128]{2,1,0:T(8,128)(2,1)}, bf16[2,448,128]{2,1,0:T(8,128)(2,1)}, u32[]{:S(2)}, u32[]{:S(2)}) %collective-permute-start.6) | collective-permute-done | bytes 229408 | tf_op jit(solution)/shard_map/ppermute | solution.py:417
  212.3 5.0 %collective-permute-done.7 = bf16[2,448,128]{2,1,0:T(8,128)(2,1)} collective-permute-done((bf16[2,448,128]{2,1,0:T(8,128)(2,1)}, bf16[2,448,128]{2,1,0:T(8,128)(2,1)}, u32[]{:S(2)}, u32[]{:S(2)}) %collective-permute-start.7) | collective-permute-done | bytes 229408 | tf_op jit(solution)/shard_map/ppermute | solution.py:417
  217.3 2.0 fusion.3
  219.3 7.4 %all-to-all-start.4 = ((bf16[16,56,128]{2,1,0:T(8,128)(2,1)}), bf16[16,56,128]{2,1,0:T(8,128)(2,1)S(1)}, u32[]{:S(2)}, u32[]{:S(2)}) async-start(bf16[16,56,128]{2,1,0:T(8,128)(2,1)} %bitcast.58), calls=%async_computation.4 | async-start | bytes 458752 | tf_op jit(solution)/shard_map/all_to_all | solution.py:515
  226.7 2.6 %collected.1 = (f32[256,128]{1,0:T(8,128)}, bf16[256,128]{1,0:T(8,128)(2,1)}, bf16[256,128]{1,0:T(8,128)(2,1)}, bf16[256,128]{1,0:T(8,128)(2,1)}) custom-call(s32[64]{0:T(128)} %reduce.picks_ref, s32[2]{0:T(128)} %bitcast.67, s32[1]{0:T(128)S(6)} %copy.52.count_ref, s32[1]{0:T(128)} %bitcast.me_ref, bf16[64,96,128]{2,1,0:T(8,128)(2,1)} %copy-done.1), custom_call_target="tpu_custom_call" | custom-call | tf_op jit(solution)/shard_map/collected/pallas_call | solution.py:334
  229.3 0.6 collective-permute-start.10
  229.9 2.7 %collective-permute-start.11 = (bf16[256,128]{1,0:T(8,128)(2,1)}, bf16[256,128]{1,0:T(8,128)(2,1)S(1)}, u32[]{:S(2)}, u32[]{:S(2)}) collective-permute-start(bf16[256,128]{1,0:T(8,128)(2,1)} %get-tuple-element.34), channel_id=1, source_target_pairs={{0,3},{1,0},{2,1},{3,2},{4,7},{5,4},{6,5},{7,6},{8,11},{9,8},{10,9... | collective-permute-start | bytes 196616 | tf_op jit(solution)/shard_map/ppermute | solution.py:417
  232.7 2.5 %collective-permute-done.10 = bf16[256,128]{1,0:T(8,128)(2,1)S(1)} collective-permute-done((bf16[256,128]{1,0:T(8,128)(2,1)}, bf16[256,128]{1,0:T(8,128)(2,1)S(1)}, u32[]{:S(2)}, u32[]{:S(2)}) %collective-permute-start.10) | collective-permute-done | bytes 65568 | tf_op jit(solution)/shard_map/ppermute | solution.py:417
  235.3 1.2 collective-permute-done.11
  236.5 1.8 collective-permute-done.9
  238.3 1.6 convert_add_fusion.1
  (32 shorter events, 1.4 us)
Async XLA Ops:
  0.6 76.0 %copy-start = (f32[128,13]{0,1:T(8,128)S(1)}, f32[128,13]{0,1:T(8,128)}, u32[]{:S(2)}) copy-start(f32[128,13]{0,1:T(8,128)} %param.22) | copy-start | bytes 19972
  0.6 50.2 %copy-start.8 = (s32[128]{0:T(128)S(1)}, s32[128]{0:T(128)}, u32[]{:S(2)}) copy-start(s32[128]{0:T(128)} %param.23) | copy-start | bytes 1540
  0.7 51.0 %copy-start.5 = (f32[3456]{0:T(1024)S(1)}, f32[3456]{0:T(1024)}, u32[]{:S(2)}) copy-start(f32[3456]{0:T(1024)} %param.18) | copy-start | bytes 41476
  0.7 51.6 %copy-start.6 = (f32[3456]{0:T(1024)S(1)}, f32[3456]{0:T(1024)}, u32[]{:S(2)}) copy-start(f32[3456]{0:T(1024)} %param.19) | copy-start | bytes 41476
  26.9 50.7 %collective-permute-start = (bf16[1024,128]{1,0:T(8,128)(2,1)S(1)}, bf16[1024,128]{1,0:T(8,128)(2,1)S(1)}, u32[]{:S(2)}, u32[]{:S(2)}) collective-permute-start(bf16[1024,128]{1,0:T(8,128)(2,1)S(1)} %bitcast.54), channel_id=1, source_target_pairs={{0,1},{1,2},{2,3},{3,0},{4,5},{5,6},{6,7},{7,4},{8,9},{9,10},{10,1... | collective-permute-start | bytes 786440 | tf_op jit(solution)/shard_map/ppermute | solution.py:417
  28.4 49.2 %collective-permute-start.1 = (bf16[1024,128]{1,0:T(8,128)(2,1)S(1)}, bf16[1024,128]{1,0:T(8,128)(2,1)S(1)}, u32[]{:S(2)}, u32[]{:S(2)}) collective-permute-start(bf16[1024,128]{1,0:T(8,128)(2,1)S(1)} %bitcast.55), channel_id=1, source_target_pairs={{0,2},{1,3},{2,0},{3,1},{4,6},{5,7},{6,4},{7,5},{8,10},{9,11},{10,... | collective-permute-start | bytes 786440 | tf_op jit(solution)/shard_map/ppermute | solution.py:417
  31.3 46.3 %collective-permute-start.2 = (bf16[1024,128]{1,0:T(8,128)(2,1)S(1)}, bf16[1024,128]{1,0:T(8,128)(2,1)S(1)}, u32[]{:S(2)}, u32[]{:S(2)}) collective-permute-start(bf16[1024,128]{1,0:T(8,128)(2,1)S(1)} %bitcast.56), channel_id=1, source_target_pairs={{0,3},{1,0},{2,1},{3,2},{4,7},{5,4},{6,5},{7,6},{8,11},{9,8},{10,9... | collective-permute-start | bytes 786440 | tf_op jit(solution)/shard_map/ppermute | solution.py:417
  42.2 14.3 %all-to-all-start.1 = ((s32[64,1,1]{2,1,0:T(1,128)}), s32[64,1,1]{2,1,0:T(1,128)S(1)}, u32[]{:S(2)}, u32[]{:S(2)}) async-start(s32[64,1,1]{2,1,0:T(1,128)} %copy.33), calls=%async_computation.1 | async-start | bytes 65536 | tf_op jit(solution)/shard_map/all_to_all | solution.py:452
  60.1 44.2 %all-to-all-start.2 = ((bf16[64,32,128]{2,1,0:T(8,128)(2,1)}), bf16[64,32,128]{2,1,0:T(8,128)(2,1)S(1)}, u32[]{:S(2)}, u32[]{:S(2)}) async-start(bf16[64,32,128]{2,1,0:T(8,128)(2,1)} %served_rows.1), calls=%async_computation.2 | async-start | bytes 1048576 | tf_op jit(solution)/shard_map/all_to_all | solution.py:455
  66.8 9.8 %copy-start.7 = (f32[13,128]{1,0:T(8,128)S(1)}, f32[13,128]{1,0:T(8,128)}, u32[]{:S(2)}) copy-start(f32[13,128]{1,0:T(8,128)} %param.20) | copy-start | bytes 19972
  66.8 9.8 %copy-start.9 = (f32[128]{0:T(128)S(1)}, f32[128]{0:T(128)}, u32[]{:S(2)}) copy-start(f32[128]{0:T(128)} %param.21) | copy-start | bytes 1540
  104.3 0.8 copy-start.2
  144.5 74.8 %all-to-all-start.3 = ((bf16[64,96,128]{2,1,0:T(8,128)(2,1)}), bf16[64,96,128]{2,1,0:T(8,128)(2,1)S(1)}, u32[]{:S(2)}, u32[]{:S(2)}) async-start(bf16[64,96,128]{2,1,0:T(8,128)(2,1)} %scatter_rows.1), calls=%async_computation.3 | async-start | bytes 3145728 | tf_op jit(solution)/shard_map/all_to_all | solution.py:487
  154.9 43.5 %collective-permute-start.3 = (bf16[2,1792,128]{2,1,0:T(8,128)(2,1)}, bf16[2,1792,128]{2,1,0:T(8,128)(2,1)S(1)}, u32[]{:S(2)}, u32[]{:S(2)}) collective-permute-start(bf16[2,1792,128]{2,1,0:T(8,128)(2,1)} %get-tuple-element.24), channel_id=1, source_target_pairs={{0,1},{1,2},{2,3},{3,0},{4,5},{5,6},{6,7},{7,4},{8,9},{9,10},{10,1... | collective-permute-start | bytes 2752520 | tf_op jit(solution)/shard_map/ppermute | solution.py:417
  155.6 42.8 %collective-permute-start.4 = (bf16[2,1792,128]{2,1,0:T(8,128)(2,1)}, bf16[2,1792,128]{2,1,0:T(8,128)(2,1)S(1)}, u32[]{:S(2)}, u32[]{:S(2)}) collective-permute-start(bf16[2,1792,128]{2,1,0:T(8,128)(2,1)} %get-tuple-element.25), channel_id=1, source_target_pairs={{0,2},{1,3},{2,0},{3,1},{4,6},{5,7},{6,4},{7,5},{8,10},{9,11},{10,... | collective-permute-start | bytes 2752520 | tf_op jit(solution)/shard_map/ppermute | solution.py:417
  156.4 42.8 %collective-permute-start.5 = (bf16[2,1792,128]{2,1,0:T(8,128)(2,1)}, bf16[2,1792,128]{2,1,0:T(8,128)(2,1)}, u32[]{:S(2)}, u32[]{:S(2)}) collective-permute-start(bf16[2,1792,128]{2,1,0:T(8,128)(2,1)} %get-tuple-element.26), channel_id=1, source_target_pairs={{0,3},{1,0},{2,1},{3,2},{4,7},{5,4},{6,5},{7,6},{8,11},{9,8},{10,9... | collective-permute-start | bytes 2752520 | tf_op jit(solution)/shard_map/ppermute | solution.py:417
  198.4 0.9 copy-start.3
  198.4 1.2 copy-start.4
  203.2 9.1 %collective-permute-start.6 = (bf16[2,448,128]{2,1,0:T(8,128)(2,1)}, bf16[2,448,128]{2,1,0:T(8,128)(2,1)}, u32[]{:S(2)}, u32[]{:S(2)}) collective-permute-start(bf16[2,448,128]{2,1,0:T(8,128)(2,1)} %get-tuple-element.35), channel_id=1, source_target_pairs={{0,8},{8,16},{16,24},{24,0},{1,9},{9,17},{17,25},{25,1},{2,10},{10... | collective-permute-start | bytes 688136 | tf_op jit(solution)/shard_map/ppermute | solution.py:417
  204.7 12.6 %collective-permute-start.7 = (bf16[2,448,128]{2,1,0:T(8,128)(2,1)}, bf16[2,448,128]{2,1,0:T(8,128)(2,1)}, u32[]{:S(2)}, u32[]{:S(2)}) collective-permute-start(bf16[2,448,128]{2,1,0:T(8,128)(2,1)} %get-tuple-element.37), channel_id=1, source_target_pairs={{0,16},{8,24},{16,0},{24,8},{1,17},{9,25},{17,1},{25,9},{2,18},{10... | collective-permute-start | bytes 688136 | tf_op jit(solution)/shard_map/ppermute | solution.py:417
  207.4 10.0 %collective-permute-start.8 = (bf16[2,448,128]{2,1,0:T(8,128)(2,1)}, bf16[2,448,128]{2,1,0:T(8,128)(2,1)}, u32[]{:S(2)}, u32[]{:S(2)}) collective-permute-start(bf16[2,448,128]{2,1,0:T(8,128)(2,1)} %get-tuple-element.36), channel_id=1, source_target_pairs={{0,24},{8,0},{16,8},{24,16},{1,25},{9,1},{17,9},{25,17},{2,26},{10... | collective-permute-start | bytes 688136 | tf_op jit(solution)/shard_map/ppermute | solution.py:417
  219.3 7.4 %copy-start.1 = (bf16[64,96,128]{2,1,0:T(8,128)(2,1)}, bf16[64,96,128]{2,1,0:T(8,128)(2,1)S(1)}, u32[]{:S(2)}) copy-start(bf16[64,96,128]{2,1,0:T(8,128)(2,1)S(1)} %all-to-all-done.3.back_ref) | copy-start | bytes 4718596
  219.3 20.5 %all-to-all-start.4 = ((bf16[16,56,128]{2,1,0:T(8,128)(2,1)}), bf16[16,56,128]{2,1,0:T(8,128)(2,1)S(1)}, u32[]{:S(2)}, u32[]{:S(2)}) async-start(bf16[16,56,128]{2,1,0:T(8,128)(2,1)} %bitcast.58), calls=%async_computation.4 | async-start | bytes 458752 | tf_op jit(solution)/shard_map/all_to_all | solution.py:515
  229.3 6.0 %collective-permute-start.10 = (bf16[256,128]{1,0:T(8,128)(2,1)}, bf16[256,128]{1,0:T(8,128)(2,1)S(1)}, u32[]{:S(2)}, u32[]{:S(2)}) collective-permute-start(bf16[256,128]{1,0:T(8,128)(2,1)} %get-tuple-element.33), channel_id=1, source_target_pairs={{0,2},{1,3},{2,0},{3,1},{4,6},{5,7},{6,4},{7,5},{8,10},{9,11},{10,... | collective-permute-start | bytes 196616 | tf_op jit(solution)/shard_map/ppermute | solution.py:417
  229.9 6.5 %collective-permute-start.11 = (bf16[256,128]{1,0:T(8,128)(2,1)}, bf16[256,128]{1,0:T(8,128)(2,1)S(1)}, u32[]{:S(2)}, u32[]{:S(2)}) collective-permute-start(bf16[256,128]{1,0:T(8,128)(2,1)} %get-tuple-element.34), channel_id=1, source_target_pairs={{0,3},{1,0},{2,1},{3,2},{4,7},{5,4},{6,5},{7,6},{8,11},{9,8},{10,9... | collective-permute-start | bytes 196616 | tf_op jit(solution)/shard_map/ppermute | solution.py:417
  232.6 5.7 %collective-permute-start.9 = (bf16[256,128]{1,0:T(8,128)(2,1)}, bf16[256,128]{1,0:T(8,128)(2,1)S(1)}, u32[]{:S(2)}, u32[]{:S(2)}) collective-permute-start(bf16[256,128]{1,0:T(8,128)(2,1)} %get-tuple-element.32), channel_id=1, source_target_pairs={{0,1},{1,2},{2,3},{3,0},{4,5},{5,6},{6,7},{7,4},{8,9},{9,10},{10,1... | collective-permute-start | bytes 196616 | tf_op jit(solution)/shard_map/ppermute | solution.py:417
